TPU v7x, 32 devices: a whole 2x2x4 slice. The times are simulated.
32 devices in a mesh: region: 8 (over z, x), band: 4 (over y, core).
Axes of the slice: x: 2, y: 2, z: 4, core: 2. Of those that a mesh axis runs over, the one named last changes fastest.
Arguments:
- probes: bfloat16 [4, 4, 512, 8192], P(None, None, 'band', 'region'), may hold values from -5 to 5
- filter_taps: float32 [2, 2, 17], replicated, may hold values from 0.02 to 1
- mixing: float32 [2, 4, 4], replicated, as said below
- nugget: float32 [4], replicated, may hold values from 0.3 to 1.5
- land_span: int32 [2, 512, 8], P(None, 'band', 'region'), may hold values from 0 to 1024, as said below
Outputs:
- covariance_probes: bfloat16 [4, 4, 512, 8192], P(None, None, 'band', 'region')
- quadratic: float32 [4, 3], replicated
Inputs may be any that keep to these rules, and one draw needn't show every extreme that they name: Row r of region block b has land in the columns land_span[0, r, b] to land_span[1, r, b] - 1 of the block; land_span[0] <= land_span[1] everywhere. `mixing`: each of the 2 matrices is symmetric positive definite.
All inputs are finite; a program needn't handle non-finite values.
Results may differ from a plain program's by a relative error of at most 0.0062.
Values may be sent and summed in bfloat16 or wider, within the bound.
No kernel may reach another device: no remote copies, remote signals or barrier semaphores. Data moves between devices by JAX's collectives and lax.ppermute only.
A program may use at most 128 MiB of HBM per device.

v0:
```python
import functools

import jax
import jax.numpy as jnp
from jax import lax
from jax.experimental import pallas as pl
from jax.experimental.pallas import tpu as pltpu
from jax.sharding import PartitionSpec as P

LANES = 128
BF16 = jnp.bfloat16
F32 = jnp.float32


def bounds_by_row(span_ref):
    out = []
    for entry in range(2):
        line = jnp.broadcast_to(span_ref[entry].astype(F32), (LANES, LANES))
        out.append(line.T)
    return out


def land_tile(low, high, first_col):
    column = (lax.broadcasted_iota(jnp.int32, low.shape, 1) + first_col).astype(F32)
    return ((column >= low) & (column < high)).astype(F32).astype(BF16)


def pack_kernel(half, span_ref, west_ref, east_ref, top_ref, bottom_ref, left_ref, right_ref, up_ref, down_ref):
    probes, variables, rows, _ = west_ref.shape
    cols = top_ref.shape[3]
    planes = probes * variables
    per_group = LANES // half
    low, high = bounds_by_row(span_ref)
    first = land_tile(low, high, 0)
    last = land_tile(low, high, cols - LANES)
    for group in range(left_ref.shape[0]):
        heads, tails = [], []
        for plane in range(group * per_group, min(planes, (group + 1) * per_group)):
            at = (plane // variables, plane % variables)
            heads.append((west_ref[at] * first)[:, :half])
            tails.append((east_ref[at] * last)[:, LANES - half :])
        left_ref[group] = jnp.concatenate(heads, axis=1)
        right_ref[group] = jnp.concatenate(tails, axis=1)
    for tile in range(cols // LANES):
        lanes = slice(tile * LANES, (tile + 1) * LANES)
        above = land_tile(low[:half], high[:half], tile * LANES)
        below = land_tile(low[rows - half :], high[rows - half :], tile * LANES)
        up_ref[:, :, :, lanes] = top_ref[:, :, :, lanes] * above[None, None]
        down_ref[:, :, :, lanes] = bottom_ref[:, :, :, lanes] * below[None, None]


def pack(probes, span, half):
    count, variables, rows, cols = probes.shape
    groups = count * variables * half // LANES
    lead = (count, variables)
    full = lambda shape: pl.BlockSpec(shape, lambda _: (0,) * len(shape))
    edge = jax.ShapeDtypeStruct((groups, rows, LANES), BF16)
    strip = jax.ShapeDtypeStruct((*lead, half, cols), BF16)
    return pl.pallas_call(
        functools.partial(pack_kernel, half),
        grid=(1,),
        out_shape=(edge, edge, strip, strip),
        in_specs=[
            full(span.shape),
            pl.BlockSpec((*lead, rows, LANES), lambda _: (0, 0, 0, 0)),
            pl.BlockSpec((*lead, rows, LANES), lambda _: (0, 0, 0, cols // LANES - 1)),
            pl.BlockSpec((*lead, half, cols), lambda _: (0, 0, 0, 0)),
            pl.BlockSpec((*lead, half, cols), lambda _: (0, 0, rows // half - 1, 0)),
        ],
        out_specs=(full(edge.shape), full(edge.shape), full(strip.shape), full(strip.shape)),
        compiler_params=pltpu.CompilerParams(vmem_limit_bytes=24 << 20),
        name="pack",
    )(span, probes, probes, probes, probes)


def table_kernel(taps_ref, across_ref, downward_ref):
    kernels, _, count = taps_ref.shape
    half = count - 1

    def toeplitz(kernel, which, distance):
        table = jnp.zeros(distance.shape, F32)
        for tap in range(count):
            table = jnp.where(distance == tap, taps_ref[kernel, which, tap], table)
        return table.astype(BF16)

    for kernel in range(kernels):
        shape = (across_ref.shape[0], LANES)
        gap = lax.broadcasted_iota(jnp.int32, shape, 0) - lax.broadcasted_iota(jnp.int32, shape, 1)
        across_ref[:, kernel * LANES : (kernel + 1) * LANES] = toeplitz(kernel, 0, jnp.abs(gap - half))
        shape = downward_ref.shape[1:]
        gap = lax.broadcasted_iota(jnp.int32, shape, 1) - lax.broadcasted_iota(jnp.int32, shape, 0)
        downward_ref[kernel] = toeplitz(kernel, 1, jnp.abs(gap - half))


def tables(taps, rows):
    kernels, _, count = taps.shape
    return pl.pallas_call(
        table_kernel,
        out_shape=(
            jax.ShapeDtypeStruct((2 * LANES, kernels * LANES), BF16),
            jax.ShapeDtypeStruct((kernels, rows, rows + 2 * (count - 1)), BF16),
        ),
        in_specs=[pl.BlockSpec(memory_space=pltpu.SMEM)],
        name="tables",
    )(taps)


def main_kernel(
    half,
    mixing_ref,
    nugget_ref,
    span_ref,
    across_ref,
    downward_ref,
    x_ref,
    west_ref,
    east_ref,
    north_ref,
    south_ref,
    above_ref,
    below_ref,
    out_ref,
    quad_ref,
    land_ref,
    ext_ref,
    interior_ref,
    sums_ref,
):
    probe = pl.program_id(0)
    variables, rows, cols = x_ref.shape[1:]
    kernels = downward_ref.shape[0]
    tiles = cols // LANES
    tall = rows + 2 * half

    @pl.when(probe == 0)
    def _():
        low, high = bounds_by_row(span_ref)
        for tile in range(tiles):
            land_ref[:, tile * LANES : (tile + 1) * LANES] = land_tile(low, high, tile * LANES)

    groups = west_ref.shape[0]
    per_group = LANES // half // variables
    group, slot = probe // per_group, probe % per_group

    def side(ref, index):
        block = ref[index].astype(F32)
        return pltpu.roll(block, (per_group - slot) * (half * variables) % LANES, 1)

    def extend(rows_at, height, tile_of, west, east):
        lane = lax.broadcasted_iota(jnp.int32, (height, LANES), 1)
        for v in range(variables):
            back = LANES - half * v
            before = pltpu.roll(west, back % LANES, 1)
            for tile in range(tiles):
                moved = pltpu.roll(tile_of(v, tile).astype(F32), half, 1)
                ext_ref[v, rows_at : rows_at + height, tile * LANES : (tile + 1) * LANES] = jnp.where(
                    lane < half, before, moved
                ).astype(BF16)
                before = moved
            after = pltpu.roll(east, (back + half) % LANES, 1)
            final = jnp.where(lane < half, before, jnp.where(lane < 2 * half, after, 0.0))
            ext_ref[v, rows_at : rows_at + height, cols : cols + LANES] = final.astype(BF16)

    def lanes_of(tile):
        return slice(tile * LANES, (tile + 1) * LANES)

    extend(
        half,
        rows,
        lambda v, t: x_ref[0, v, :, lanes_of(t)] * land_ref[:, lanes_of(t)],
        side(west_ref, group),
        side(east_ref, group),
    )
    extend(0, half, lambda v, t: north_ref[0, v, :, lanes_of(t)], side(above_ref, group), side(above_ref, groups + group))
    extend(
        half + rows, half, lambda v, t: south_ref[0, v, :, lanes_of(t)], side(below_ref, group), side(below_ref, groups + group)
    )

    for tile in range(tiles):
        window = ext_ref[:, :, tile * LANES : (tile + 2) * LANES].reshape(variables * tall, 2 * LANES)
        both = jnp.dot(window, across_ref[...], preferred_element_type=F32).astype(BF16)
        for kernel in range(kernels):
            interior_ref[kernel, :, :, lanes_of(tile)] = both[:, lanes_of(kernel)].reshape(variables, tall, LANES)

    sums = [jnp.zeros((8, LANES), F32) for _ in range(kernels + 1)]
    wide = 2 * LANES
    for chunk in range(cols // wide):
        span = slice(chunk * wide, (chunk + 1) * wide)
        smooth = [
            [
                jnp.dot(downward_ref[kernel], interior_ref[kernel, w, :, span], preferred_element_type=F32)
                for w in range(variables)
            ]
            for kernel in range(kernels)
        ]
        land = land_ref[:, span].astype(F32)
        for v in range(variables):
            local = (x_ref[0, v, :, span] * land_ref[:, span]).astype(F32)
            total = nugget_ref[v] * local
            parts = [total * local]
            for kernel in range(kernels):
                term = mixing_ref[kernel, v, 0] * smooth[kernel][0]
                for w in range(1, variables):
                    term = term + mixing_ref[kernel, v, w] * smooth[kernel][w]
                parts.append(term * local)
                total = total + term
            out_ref[0, v, :, span] = (total * land).astype(BF16)
            for k, part in enumerate(parts[1:] + parts[:1]):
                folded = jnp.sum(part.reshape(rows // 8, 8, wide), axis=0)
                sums[k] = sums[k] + folded[:, :LANES] + folded[:, LANES:]
    for k in range(kernels + 1):
        sums_ref[probe, k] = sums[k]

    @pl.when(probe == pl.num_programs(0) - 1)
    def _():
        lane = lax.broadcasted_iota(jnp.int32, quad_ref.shape, 1)
        line = jnp.zeros(quad_ref.shape, F32)
        for p in range(sums_ref.shape[0]):
            for k in range(kernels + 1):
                line = jnp.where(lane == p * (kernels + 1) + k, jnp.sum(sums_ref[p, k]), line)
        quad_ref[...] = line


def main(mixing, nugget, span, across, downward, probes, west, east, north, south, above, below, half, devices):
    count, variables, rows, cols = probes.shape
    kernels = downward.shape[0]
    tall = rows + 2 * half
    full = lambda a: pl.BlockSpec(a.shape, lambda p: (0,) * a.ndim)
    one = lambda height: pl.BlockSpec((1, variables, height, cols), lambda p: (p, 0, 0, 0))
    smem = pl.BlockSpec(memory_space=pltpu.SMEM)
    return pl.pallas_call(
        functools.partial(main_kernel, half),
        grid=(count,),
        out_shape=(jax.ShapeDtypeStruct(probes.shape, BF16), jax.ShapeDtypeStruct((devices, LANES), F32)),
        in_specs=[
            smem,
            smem,
            full(span),
            full(across),
            full(downward),
            one(rows),
            full(west),
            full(east),
            one(half),
            one(half),
            full(above),
            full(below),
        ],
        out_specs=(one(rows), pl.BlockSpec((devices, LANES), lambda p: (0, 0))),
        scratch_shapes=[
            pltpu.VMEM((rows, cols), BF16),
            pltpu.VMEM((variables, tall, cols + LANES), BF16),
            pltpu.VMEM((kernels, variables, tall, cols), BF16),
            pltpu.VMEM((count, kernels + 1, 8, LANES), F32),
        ],
        compiler_params=pltpu.CompilerParams(vmem_limit_bytes=40 << 20),
        name="covariance",
    )(mixing, nugget, span, across, downward, probes, west, east, north, south, above, below)


def per_device(probes, filter_taps, mixing, nugget, land_span):
    count, variables, rows, cols = probes.shape
    kernels = filter_taps.shape[0]
    half = filter_taps.shape[2] - 1
    regions, bands = lax.axis_size("region"), lax.axis_size("band")
    east_of = [(i, (i + 1) % regions) for i in range(regions)]
    west_of = [((i + 1) % regions, i) for i in range(regions)]
    south_of = [(i, i + 1) for i in range(bands - 1)]
    north_of = [(i + 1, i) for i in range(bands - 1)]

    span = land_span.reshape(2, 1, rows)
    left, right, up, down = pack(probes, span, half)
    west = lax.ppermute(right, "region", east_of)
    east = lax.ppermute(left, "region", west_of)
    north = lax.ppermute(down, "band", south_of)
    south = lax.ppermute(up, "band", north_of)
    across, downward = tables(filter_taps, rows)
    above = lax.ppermute(jnp.concatenate([west[:, rows - half :], east[:, rows - half :]]), "band", south_of)
    below = lax.ppermute(jnp.concatenate([west[:, :half], east[:, :half]]), "band", north_of)
    output, quads = main(
        mixing, nugget, span, across, downward, probes, west, east, north, south, above, below, half, regions * bands
    )
    shares = lax.all_to_all(quads, ("region", "band"), 0, 0, tiled=True)
    quadratic = jnp.sum(shares, axis=0)[: count * (kernels + 1)].reshape(count, kernels + 1)
    return output, quadratic / (bands * rows * cols)


def solution(mesh):
    in_specs = (P(None, None, "band", "region"), P(), P(), P(), P(None, "band", "region"))
    out_specs = (P(None, None, "band", "region"), P())
    return jax.shard_map(
        per_device, mesh=mesh, in_specs=in_specs, out_specs=out_specs, check_vma=False
    )
```

profile of v0, /device:TPU:0, one launch (start us, length us, event | category | flops | bytes accessed | tf_op | source)
XLA Modules:
  0.0 54.0 jit_solution(15190373368720495354)
XLA Ops:
  0.6 0.0 copy-start
  0.6 2.2 %copy-done = bf16[4,4,128,1024]{3,2,1,0:T(8,128)(2,1)S(1)} copy-done((bf16[4,4,128,1024]{3,2,1,0:T(8,128)(2,1)S(1)}, bf16[4,4,128,1024]{3,2,1,0:T(8,128)(2,1)}, u32[]{:S(2)}) %copy-start) | copy-done | bytes 4194328
  2.8 0.0 copy-start.5
  2.8 0.7 %copy-done.5 = s32[2,128,1]{1,2,0:T(1,128)S(1)} copy-done((s32[2,128,1]{1,2,0:T(1,128)S(1)}, s32[2,128,1]{1,2,0:T(1,128)}, u32[]{:S(2)}) %copy-start.5) | copy-done | bytes 1048
  3.5 0.0 copy-start.4
  3.5 0.0 copy-start.6
  3.5 0.0 copy-start.7
  3.5 0.8 %pack.1 = (bf16[2,128,128]{2,1,0:T(8,128)(2,1)S(1)}, bf16[2,128,128]{2,1,0:T(8,128)(2,1)S(1)}, bf16[4,4,16,1024]{3,2,1,0:T(8,128)(2,1)S(1)}, bf16[4,4,16,1024]{3,2,1,0:T(8,128)(2,1)S(1)}) custom-call(s32[2,1,128]{2,1,0:T(1,128)S(1)} %bitcast.5, bf16[4,4,128,1024]{3,2,1,0:T(8,128)(2,1)S(1)} %copy-done, bf16[4,4,128,1024]{3,2,1,0:T(8,128)(2,1)S(1)} %copy-done, ...), custom_call_target="tpu_custom_call" | custom-call | tf_op jit(solution)/shard_map/pack/pallas_call | solution.py:59
  4.3 3.0 %collective-permute-start = (bf16[2,128,128]{2,1,0:T(8,128)(2,1)S(1)}, bf16[2,128,128]{2,1,0:T(8,128)(2,1)S(1)}, u32[]{:S(2)}, u32[]{:S(2)}) collective-permute-start(bf16[2,128,128]{2,1,0:T(8,128)(2,1)S(1)} %get-tuple-element.12), channel_id=1, source_target_pairs={{0,4},{4,8},{8,12},{12,16},{16,20},{20,24},{24,28},{28,0},{1,5},{5... | collective-permute-start | bytes 196616 | tf_op jit(solution)/shard_map/ppermute | solution.py:273
  7.3 3.1 %collective-permute-start.1 = (bf16[2,128,128]{2,1,0:T(8,128)(2,1)S(1)}, bf16[2,128,128]{2,1,0:T(8,128)(2,1)S(1)}, u32[]{:S(2)}, u32[]{:S(2)}) collective-permute-start(bf16[2,128,128]{2,1,0:T(8,128)(2,1)S(1)} %get-tuple-element.13), channel_id=1, source_target_pairs={{4,0},{8,4},{12,8},{16,12},{20,16},{24,20},{28,24},{0,28},{5,1},{9... | collective-permute-start | bytes 196616 | tf_op jit(solution)/shard_map/ppermute | solution.py:274
  10.4 1.5 %collective-permute-start.2 = (bf16[4,4,16,1024]{3,2,1,0:T(8,128)(2,1)S(1)}, bf16[4,4,16,1024]{3,2,1,0:T(8,128)(2,1)S(1)}, u32[]{:S(2)}, u32[]{:S(2)}) collective-permute-start(bf16[4,4,16,1024]{3,2,1,0:T(8,128)(2,1)S(1)} %get-tuple-element.14), channel_id=1, source_target_pairs={{0,1},{1,2},{2,3},{4,5},{5,6},{6,7},{8,9},{9,10},{10,11},{12,13},{... | collective-permute-start | bytes 1572872 | tf_op jit(solution)/shard_map/ppermute | solution.py:275
  11.9 1.3 %collective-permute-start.3 = (bf16[4,4,16,1024]{3,2,1,0:T(8,128)(2,1)S(1)}, bf16[4,4,16,1024]{3,2,1,0:T(8,128)(2,1)S(1)}, u32[]{:S(2)}, u32[]{:S(2)}) collective-permute-start(bf16[4,4,16,1024]{3,2,1,0:T(8,128)(2,1)S(1)} %get-tuple-element.15), channel_id=1, source_target_pairs={{1,0},{2,1},{3,2},{5,4},{6,5},{7,6},{9,8},{10,9},{11,10},{13,12},{... | collective-permute-start | bytes 1572872 | tf_op jit(solution)/shard_map/ppermute | solution.py:276
  13.2 0.0 collective-permute-done.west_ref
  13.2 0.0 collective-permute-done.1.east_ref
  13.3 4.7 %collective-permute-start.4 = (bf16[4,16,128]{2,1,0:T(8,128)(2,1)S(1)}, bf16[4,16,128]{2,1,0:T(8,128)(2,1)S(1)}, u32[]{:S(2)}, u32[]{:S(2)}) collective-permute-start(bf16[4,16,128]{2,1,0:T(8,128)(2,1)S(1)} %pad_maximum_fusion), channel_id=1, source_target_pairs={{0,1},{1,2},{2,3},{4,5},{5,6},{6,7},{8,9},{9,10},{10,11},{12,13},{... | collective-permute-start | bytes 49160 | tf_op jit(solution)/shard_map/ppermute | solution.py:278
  18.0 1.3 %collective-permute-start.5 = (bf16[4,16,128]{2,1,0:T(8,128)(2,1)S(1)}, bf16[4,16,128]{2,1,0:T(8,128)(2,1)S(1)}, u32[]{:S(2)}, u32[]{:S(2)}) collective-permute-start(bf16[4,16,128]{2,1,0:T(8,128)(2,1)S(1)} %pad_maximum_fusion.1), channel_id=1, source_target_pairs={{1,0},{2,1},{3,2},{5,4},{6,5},{7,6},{9,8},{10,9},{11,10},{13,12},{... | collective-permute-start | bytes 49160 | tf_op jit(solution)/shard_map/ppermute | solution.py:279
  19.3 1.8 %tables.1 = (bf16[256,256]{1,0:T(8,128)(2,1)}, bf16[2,128,160]{2,1,0:T(8,128)(2,1)}) custom-call(f32[2,2,17]{2,1,0:T(2,128)} %taps_ref.1), custom_call_target="tpu_custom_call" | custom-call | tf_op jit(solution)/shard_map/tables/pallas_call | solution.py:97
  21.0 0.0 collective-permute-done.4.above_ref
  21.1 1.3 %collective-permute-done.5.below_ref = bf16[4,16,128]{2,1,0:T(8,128)(2,1)S(1)} collective-permute-done((bf16[4,16,128]{2,1,0:T(8,128)(2,1)S(1)}, bf16[4,16,128]{2,1,0:T(8,128)(2,1)S(1)}, u32[]{:S(2)}, u32[]{:S(2)}) %collective-permute-start.5) | collective-permute-done | bytes 16416 | tf_op jit(solution)/shard_map/ppermute | solution.py:279
  22.3 0.0 collective-permute-done.2.north_ref
  22.3 0.0 collective-permute-done.3.south_ref
  22.3 0.0 copy-done.4
  22.3 0.0 copy-done.6
  22.3 0.0 copy-done.7
  22.3 0.0 copy-start.1
  22.4 2.2 %copy-done.1 = bf16[4,4,128,1024]{3,2,1,0:T(8,128)(2,1)S(1)} copy-done((bf16[4,4,128,1024]{3,2,1,0:T(8,128)(2,1)S(1)}, bf16[4,4,128,1024]{3,2,1,0:T(8,128)(2,1)}, u32[]{:S(2)}) %copy-start.1) | copy-done | bytes 4194328
  24.5 0.0 copy-start.2
  24.5 0.9 %copy-done.2 = bf16[256,256]{1,0:T(8,128)(2,1)S(1)} copy-done((bf16[256,256]{1,0:T(8,128)(2,1)S(1)}, bf16[256,256]{1,0:T(8,128)(2,1)}, u32[]{:S(2)}) %copy-start.2) | copy-done | bytes 131096
  25.4 0.0 copy-start.3
  25.4 0.9 %copy-done.3 = bf16[2,128,160]{2,1,0:T(8,128)(2,1)S(1)} copy-done((bf16[2,128,160]{2,1,0:T(8,128)(2,1)S(1)}, bf16[2,128,160]{2,1,0:T(8,128)(2,1)}, u32[]{:S(2)}) %copy-start.3) | copy-done | bytes 81944
  26.3 15.6 %covariance.1 = (bf16[4,4,128,1024]{3,2,1,0:T(8,128)(2,1)}, f32[32,128]{1,0:T(8,128)S(1)}) custom-call(f32[2,4,4]{2,1,0:T(4,128)S(1)} %copy-done.4, f32[4]{0:T(128)S(1)} %copy-done.7, s32[2,1,128]{2,1,0:T(1,128)S(1)} %bitcast.6, bf16[256,256]{1,0:T(8,128)(2,1)S(1)} %copy-done.2, bf16[2,128,160]{2,1,0:T(8,128)(2,1)S(1)} %copy-done.3, ...), custom_call_target="tpu_custom_call" | custom-call | tf_op jit(solution)/shard_map/covariance/pallas_call | solution.py:231
  41.9 11.4 %all_to_all.9 = f32[32,1,128]{2,1,0:T(1,128)S(1)} all-to-all(f32[32,1,128]{2,1,0:T(1,128)S(1)} %bitcast.4), channel_id=1, replica_groups=mesh['region'=8,'band'=4] {'region','band'}, dimensions={0} | all-to-all | bytes 32768 | tf_op jit(solution)/shard_map/all_to_all | solution.py:283
  53.3 0.1 reduce_sum.9
  53.3 0.7 %div.6 = f32[4,3]{1,0:T(4,128)} reshape(f32[12]{0:T(128)S(1)} %slice_multiply_fusion) | data formatting | bytes 96 | tf_op jit(solution)/shard_map/div | solution.py:285
  (5 shorter events, 0.0 us)
Async XLA Ops:
  0.6 2.2 %copy-start = (bf16[4,4,128,1024]{3,2,1,0:T(8,128)(2,1)S(1)}, bf16[4,4,128,1024]{3,2,1,0:T(8,128)(2,1)}, u32[]{:S(2)}) copy-start(bf16[4,4,128,1024]{3,2,1,0:T(8,128)(2,1)} %x_ref.1) | copy-start | bytes 12582916
  2.8 0.7 %copy-start.5 = (s32[2,128,1]{1,2,0:T(1,128)S(1)}, s32[2,128,1]{1,2,0:T(1,128)}, u32[]{:S(2)}) copy-start(s32[2,128,1]{1,2,0:T(1,128)} %param.9) | copy-start | bytes 3076
  3.5 18.8 %copy-start.4 = (f32[2,4,4]{2,1,0:T(4,128)S(1)}, f32[2,4,4]{2,1,0:T(4,128)}, u32[]{:S(2)}) copy-start(f32[2,4,4]{2,1,0:T(4,128)} %mixing_ref.1) | copy-start | bytes 388
  3.5 18.8 %copy-start.6 = (s32[2,128,1]{1,2,0:T(1,128)S(1)}, s32[2,128,1]{1,2,0:T(1,128)}, u32[]{:S(2)}) copy-start(s32[2,128,1]{1,2,0:T(1,128)} %param.9) | copy-start | bytes 3076
  3.5 18.8 %copy-start.7 = (f32[4]{0:T(128)S(1)}, f32[4]{0:T(128)}, u32[]{:S(2)}) copy-start(f32[4]{0:T(128)} %nugget_ref.1) | copy-start | bytes 52
  4.3 8.9 %collective-permute-start = (bf16[2,128,128]{2,1,0:T(8,128)(2,1)S(1)}, bf16[2,128,128]{2,1,0:T(8,128)(2,1)S(1)}, u32[]{:S(2)}, u32[]{:S(2)}) collective-permute-start(bf16[2,128,128]{2,1,0:T(8,128)(2,1)S(1)} %get-tuple-element.12), channel_id=1, source_target_pairs={{0,4},{4,8},{8,12},{12,16},{16,20},{20,24},{24,28},{28,0},{1,5},{5... | collective-permute-start | bytes 196616 | tf_op jit(solution)/shard_map/ppermute | solution.py:273
  7.3 5.9 %collective-permute-start.1 = (bf16[2,128,128]{2,1,0:T(8,128)(2,1)S(1)}, bf16[2,128,128]{2,1,0:T(8,128)(2,1)S(1)}, u32[]{:S(2)}, u32[]{:S(2)}) collective-permute-start(bf16[2,128,128]{2,1,0:T(8,128)(2,1)S(1)} %get-tuple-element.13), channel_id=1, source_target_pairs={{4,0},{8,4},{12,8},{16,12},{20,16},{24,20},{28,24},{0,28},{5,1},{9... | collective-permute-start | bytes 196616 | tf_op jit(solution)/shard_map/ppermute | solution.py:274
  10.4 11.9 %collective-permute-start.2 = (bf16[4,4,16,1024]{3,2,1,0:T(8,128)(2,1)S(1)}, bf16[4,4,16,1024]{3,2,1,0:T(8,128)(2,1)S(1)}, u32[]{:S(2)}, u32[]{:S(2)}) collective-permute-start(bf16[4,4,16,1024]{3,2,1,0:T(8,128)(2,1)S(1)} %get-tuple-element.14), channel_id=1, source_target_pairs={{0,1},{1,2},{2,3},{4,5},{5,6},{6,7},{8,9},{9,10},{10,11},{12,13},{... | collective-permute-start | bytes 1572872 | tf_op jit(solution)/shard_map/ppermute | solution.py:275
  11.9 10.4 %collective-permute-start.3 = (bf16[4,4,16,1024]{3,2,1,0:T(8,128)(2,1)S(1)}, bf16[4,4,16,1024]{3,2,1,0:T(8,128)(2,1)S(1)}, u32[]{:S(2)}, u32[]{:S(2)}) collective-permute-start(bf16[4,4,16,1024]{3,2,1,0:T(8,128)(2,1)S(1)} %get-tuple-element.15), channel_id=1, source_target_pairs={{1,0},{2,1},{3,2},{5,4},{6,5},{7,6},{9,8},{10,9},{11,10},{13,12},{... | collective-permute-start | bytes 1572872 | tf_op jit(solution)/shard_map/ppermute | solution.py:276
  13.3 7.8 %collective-permute-start.4 = (bf16[4,16,128]{2,1,0:T(8,128)(2,1)S(1)}, bf16[4,16,128]{2,1,0:T(8,128)(2,1)S(1)}, u32[]{:S(2)}, u32[]{:S(2)}) collective-permute-start(bf16[4,16,128]{2,1,0:T(8,128)(2,1)S(1)} %pad_maximum_fusion), channel_id=1, source_target_pairs={{0,1},{1,2},{2,3},{4,5},{5,6},{6,7},{8,9},{9,10},{10,11},{12,13},{... | collective-permute-start | bytes 49160 | tf_op jit(solution)/shard_map/ppermute | solution.py:278
  18.0 4.3 %collective-permute-start.5 = (bf16[4,16,128]{2,1,0:T(8,128)(2,1)S(1)}, bf16[4,16,128]{2,1,0:T(8,128)(2,1)S(1)}, u32[]{:S(2)}, u32[]{:S(2)}) collective-permute-start(bf16[4,16,128]{2,1,0:T(8,128)(2,1)S(1)} %pad_maximum_fusion.1), channel_id=1, source_target_pairs={{1,0},{2,1},{3,2},{5,4},{6,5},{7,6},{9,8},{10,9},{11,10},{13,12},{... | collective-permute-start | bytes 49160 | tf_op jit(solution)/shard_map/ppermute | solution.py:279
  22.3 2.2 %copy-start.1 = (bf16[4,4,128,1024]{3,2,1,0:T(8,128)(2,1)S(1)}, bf16[4,4,128,1024]{3,2,1,0:T(8,128)(2,1)}, u32[]{:S(2)}) copy-start(bf16[4,4,128,1024]{3,2,1,0:T(8,128)(2,1)} %x_ref.1) | copy-start | bytes 12582916
  24.5 0.9 %copy-start.2 = (bf16[256,256]{1,0:T(8,128)(2,1)S(1)}, bf16[256,256]{1,0:T(8,128)(2,1)}, u32[]{:S(2)}) copy-start(bf16[256,256]{1,0:T(8,128)(2,1)} %get-tuple-element.10.across_ref) | copy-start | bytes 393220
  25.4 0.9 %copy-start.3 = (bf16[2,128,160]{2,1,0:T(8,128)(2,1)S(1)}, bf16[2,128,160]{2,1,0:T(8,128)(2,1)}, u32[]{:S(2)}) copy-start(bf16[2,128,160]{2,1,0:T(8,128)(2,1)} %get-tuple-element.11.downward_ref) | copy-start | bytes 245764
where the time goes:
time: 54.4 us; the launch traced here: 54 us
  Pallas kernels  18.1 us (33%)
  starting transfers between devices  14.9 us (27%)
  blocking collectives  11.4 us (21%)
  local copies, waits for them, and re-layouts  7.53 us (14%)
  waiting for transfers between devices  1.27 us (2%)
  between operations  0.76 us (1%)
    pallas_call x1, Pallas kernels, main(): pl.pallas_call(functools.partial(main_kernel, half), grid=(count,), out_s...  15.6 us
    all_to_all x1, blocking collectives, per_device(): shares = lax.all_to_all(quads, ('region', 'band'), 0, 0, tiled=True)  11.4 us
    unnamed x16, local copies, waits for them, and re-layouts  6.86 us
    ppermute x1, starting transfers between devices, per_device(): lax.ppermute(jnp.concatenate([west[:, rows - half:], east[:, rows - half:...  4.71 us
    ppermute x1, starting transfers between devices, per_device(): east = lax.ppermute(left, 'region', west_of)  3.1 us
    ppermute x1, starting transfers between devices, per_device(): west = lax.ppermute(right, 'region', east_of)  3.02 us
    pallas_call x1, Pallas kernels, tables(): pl.pallas_call(table_kernel, out_shape=(jax.ShapeDtypeStruct((2 * LANES,...  1.76 us
    ppermute x1, starting transfers between devices, per_device(): north = lax.ppermute(down, 'band', south_of)  1.48 us
  transfers between devices with their start and end apart: 6, of which 1 were waited for; matrix products, arithmetic and copies ran while one was open for 0% of the time, Pallas kernels for 3%

commit v1 on v0

--- a/solution.py
+++ b/solution.py
@@ -10,6 +10,7 @@
 LANES = 128
 BF16 = jnp.bfloat16
 F32 = jnp.float32
+VMEM = 61 << 20
 
 
 def bounds_by_row(span_ref):
@@ -25,7 +26,9 @@
     return ((column >= low) & (column < high)).astype(F32).astype(BF16)
 
 
-def pack_kernel(half, span_ref, west_ref, east_ref, top_ref, bottom_ref, left_ref, right_ref, up_ref, down_ref):
+def pack_kernel(
+    half, odd_ref, span_ref, west_ref, east_ref, top_ref, bottom_ref, inner_ref, outer_ref, near_ref, far_ref
+):
     probes, variables, rows, _ = west_ref.shape
     cols = top_ref.shape[3]
     planes = probes * variables
@@ -33,23 +36,37 @@
     low, high = bounds_by_row(span_ref)
     first = land_tile(low, high, 0)
     last = land_tile(low, high, cols - LANES)
-    for group in range(left_ref.shape[0]):
-        heads, tails = [], []
-        for plane in range(group * per_group, min(planes, (group + 1) * per_group)):
-            at = (plane // variables, plane % variables)
-            heads.append((west_ref[at] * first)[:, :half])
-            tails.append((east_ref[at] * last)[:, LANES - half :])
-        left_ref[group] = jnp.concatenate(heads, axis=1)
-        right_ref[group] = jnp.concatenate(tails, axis=1)
-    for tile in range(cols // LANES):
-        lanes = slice(tile * LANES, (tile + 1) * LANES)
-        above = land_tile(low[:half], high[:half], tile * LANES)
-        below = land_tile(low[rows - half :], high[rows - half :], tile * LANES)
-        up_ref[:, :, :, lanes] = top_ref[:, :, :, lanes] * above[None, None]
-        down_ref[:, :, :, lanes] = bottom_ref[:, :, :, lanes] * below[None, None]
-
-
-def pack(probes, span, half):
+
+    def columns(left_ref, right_ref):
+        for group in range(left_ref.shape[0]):
+            heads, tails = [], []
+            for plane in range(group * per_group, min(planes, (group + 1) * per_group)):
+                at = (plane // variables, plane % variables)
+                heads.append((west_ref[at] * first)[:, :half])
+                tails.append((east_ref[at] * last)[:, LANES - half :])
+            left_ref[group] = jnp.concatenate(heads, axis=1)
+            right_ref[group] = jnp.concatenate(tails, axis=1)
+
+    def strips(up_ref, down_ref):
+        for tile in range(cols // LANES):
+            lanes = slice(tile * LANES, (tile + 1) * LANES)
+            above = land_tile(low[:half], high[:half], tile * LANES)
+            below = land_tile(low[rows - half :], high[rows - half :], tile * LANES)
+            up_ref[:, :, :, lanes] = top_ref[:, :, :, lanes] * above[None, None]
+            down_ref[:, :, :, lanes] = bottom_ref[:, :, :, lanes] * below[None, None]
+
+    for which, work, ends in ((0, columns, (outer_ref, inner_ref)), (1, strips, (far_ref, near_ref))):
+
+        @pl.when(odd_ref[which] == 0)
+        def _(work=work, ends=ends):
+            work(*ends)
+
+        @pl.when(odd_ref[which] != 0)
+        def _(work=work, ends=ends):
+            work(*ends[::-1])
+
+
+def pack(odd, probes, span, half):
     count, variables, rows, cols = probes.shape
     groups = count * variables * half // LANES
     lead = (count, variables)
@@ -61,6 +78,7 @@
         grid=(1,),
         out_shape=(edge, edge, strip, strip),
         in_specs=[
+            pl.BlockSpec(memory_space=pltpu.SMEM),
             full(span.shape),
             pl.BlockSpec((*lead, rows, LANES), lambda _: (0, 0, 0, 0)),
             pl.BlockSpec((*lead, rows, LANES), lambda _: (0, 0, 0, cols // LANES - 1)),
@@ -68,9 +86,9 @@
             pl.BlockSpec((*lead, half, cols), lambda _: (0, 0, rows // half - 1, 0)),
         ],
         out_specs=(full(edge.shape), full(edge.shape), full(strip.shape), full(strip.shape)),
-        compiler_params=pltpu.CompilerParams(vmem_limit_bytes=24 << 20),
+        compiler_params=pltpu.CompilerParams(vmem_limit_bytes=VMEM),
         name="pack",
-    )(span, probes, probes, probes, probes)
+    )(odd, span, probes, probes, probes, probes)
 
 
 def table_kernel(taps_ref, across_ref, downward_ref):
@@ -107,18 +125,19 @@
 
 def main_kernel(
     half,
+    odd_ref,
     mixing_ref,
     nugget_ref,
     span_ref,
     across_ref,
     downward_ref,
     x_ref,
-    west_ref,
-    east_ref,
-    north_ref,
-    south_ref,
-    above_ref,
-    below_ref,
+    inner_ref,
+    outer_ref,
+    near_ref,
+    far_ref,
+    near_corner_ref,
+    far_corner_ref,
     out_ref,
     quad_ref,
     land_ref,
@@ -138,13 +157,16 @@
         for tile in range(tiles):
             land_ref[:, tile * LANES : (tile + 1) * LANES] = land_tile(low, high, tile * LANES)
 
-    groups = west_ref.shape[0]
+    groups = inner_ref.shape[0]
     per_group = LANES // half // variables
     group, slot = probe // per_group, probe % per_group
-
-    def side(ref, index):
-        block = ref[index].astype(F32)
-        return pltpu.roll(block, (per_group - slot) * (half * variables) % LANES, 1)
+    odd_region, odd_band = odd_ref[0] != 0, odd_ref[1] != 0
+
+    def side(block):
+        return pltpu.roll(block.astype(F32), (per_group - slot) * (half * variables) % LANES, 1)
+
+    def sides(inner, outer):
+        return side(jnp.where(odd_region, inner, outer)), side(jnp.where(odd_region, outer, inner))
 
     def extend(rows_at, height, tile_of, west, east):
         lane = lax.broadcasted_iota(jnp.int32, (height, LANES), 1)
@@ -168,13 +190,18 @@
         half,
         rows,
         lambda v, t: x_ref[0, v, :, lanes_of(t)] * land_ref[:, lanes_of(t)],
-        side(west_ref, group),
-        side(east_ref, group),
+        *sides(inner_ref[group], outer_ref[group]),
     )
-    extend(0, half, lambda v, t: north_ref[0, v, :, lanes_of(t)], side(above_ref, group), side(above_ref, groups + group))
-    extend(
-        half + rows, half, lambda v, t: south_ref[0, v, :, lanes_of(t)], side(below_ref, group), side(below_ref, groups + group)
-    )
+    for rows_at, from_near in ((0, odd_band), (half + rows, jnp.logical_not(odd_band))):
+        corner = [
+            jnp.where(from_near, near_corner_ref[kind + group], far_corner_ref[kind + group]) for kind in (0, groups)
+        ]
+        extend(
+            rows_at,
+            half,
+            lambda v, t, near=from_near: jnp.where(near, near_ref[0, v, :, lanes_of(t)], far_ref[0, v, :, lanes_of(t)]),
+            *sides(*corner),
+        )
 
     for tile in range(tiles):
         window = ext_ref[:, :, tile * LANES : (tile + 2) * LANES].reshape(variables * tall, 2 * LANES)
@@ -221,7 +248,7 @@
         quad_ref[...] = line
 
 
-def main(mixing, nugget, span, across, downward, probes, west, east, north, south, above, below, half, devices):
+def main(odd, mixing, nugget, span, across, downward, probes, inner, outer, near, far, near_corner, far_corner, half, devices):
     count, variables, rows, cols = probes.shape
     kernels = downward.shape[0]
     tall = rows + 2 * half
@@ -235,16 +262,17 @@
         in_specs=[
             smem,
             smem,
+            smem,
             full(span),
             full(across),
             full(downward),
             one(rows),
-            full(west),
-            full(east),
+            full(inner),
+            full(outer),
             one(half),
             one(half),
-            full(above),
-            full(below),
+            full(near_corner),
+            full(far_corner),
         ],
         out_specs=(one(rows), pl.BlockSpec((devices, LANES), lambda p: (0, 0))),
         scratch_shapes=[
@@ -253,9 +281,9 @@
             pltpu.VMEM((kernels, variables, tall, cols), BF16),
             pltpu.VMEM((count, kernels + 1, 8, LANES), F32),
         ],
-        compiler_params=pltpu.CompilerParams(vmem_limit_bytes=40 << 20),
+        compiler_params=pltpu.CompilerParams(vmem_limit_bytes=VMEM),
         name="covariance",
-    )(mixing, nugget, span, across, downward, probes, west, east, north, south, above, below)
+    )(odd, mixing, nugget, span, across, downward, probes, inner, outer, near, far, near_corner, far_corner)
 
 
 def per_device(probes, filter_taps, mixing, nugget, land_span):
@@ -263,22 +291,41 @@
     kernels = filter_taps.shape[0]
     half = filter_taps.shape[2] - 1
     regions, bands = lax.axis_size("region"), lax.axis_size("band")
-    east_of = [(i, (i + 1) % regions) for i in range(regions)]
-    west_of = [((i + 1) % regions, i) for i in range(regions)]
-    south_of = [(i, i + 1) for i in range(bands - 1)]
-    north_of = [(i + 1, i) for i in range(bands - 1)]
-
+    pairs = {
+        "inner": [(i, i ^ 1) for i in range(regions)],
+        "outer": [(i, (i + 1 if i % 2 else i - 1) % regions) for i in range(regions)],
+        "near": [(i, i ^ 1) for i in range(bands)],
+        "far": [(i, i + 1 if i % 2 else i - 1) for i in range(1, bands - 1)],
+    }
+
+    odd = jnp.stack([lax.axis_index("region") % 2, lax.axis_index("band") % 2]).astype(jnp.int32)
     span = land_span.reshape(2, 1, rows)
-    left, right, up, down = pack(probes, span, half)
-    west = lax.ppermute(right, "region", east_of)
-    east = lax.ppermute(left, "region", west_of)
-    north = lax.ppermute(down, "band", south_of)
-    south = lax.ppermute(up, "band", north_of)
+    inner, outer, near, far = pack(odd, probes, span, half)
+    inner = lax.ppermute(inner, "region", pairs["inner"])
+    outer = lax.ppermute(outer, "region", pairs["outer"])
+    near = lax.ppermute(near, "band", pairs["near"])
+    far = lax.ppermute(far, "band", pairs["far"])
     across, downward = tables(filter_taps, rows)
-    above = lax.ppermute(jnp.concatenate([west[:, rows - half :], east[:, rows - half :]]), "band", south_of)
-    below = lax.ppermute(jnp.concatenate([west[:, :half], east[:, :half]]), "band", north_of)
+    top = jnp.concatenate([inner[:, :half], outer[:, :half]])
+    bottom = jnp.concatenate([inner[:, rows - half :], outer[:, rows - half :]])
+    near_corner = lax.ppermute(jnp.where(odd[1] != 0, top, bottom), "band", pairs["near"])
+    far_corner = lax.ppermute(jnp.where(odd[1] != 0, bottom, top), "band", pairs["far"])
     output, quads = main(
-        mixing, nugget, span, across, downward, probes, west, east, north, south, above, below, half, regions * bands
+        odd,
+        mixing,
+        nugget,
+        span,
+        across,
+        downward,
+        probes,
+        inner,
+        outer,
+        near,
+        far,
+        near_corner,
+        far_corner,
+        half,
+        regions * bands,
     )
     shares = lax.all_to_all(quads, ("region", "band"), 0, 0, tiled=True)
     quadratic = jnp.sum(shares, axis=0)[: count * (kernels + 1)].reshape(count, kernels + 1)

time: 54.4 us -> 50.4 us (0.926)
  local copies, waits for them, and re-layouts: 7.53 us -> 1.61 us
  starting transfers between devices: 14.9 us -> 10.8 us
  Pallas kernels: 18.1 us -> 21.5 us
  waiting for transfers between devices: 1.27 us -> 2.88 us
  other arithmetic: 0.07 us -> 0.62 us
    unnamed x16 -> x12, local copies, waits for them, and re-layouts: 6.86 us -> 0.94 us
    ppermute x6, starting transfers between devices: 14.9 us -> 10.8 us  [the longest x1 3.58 us: per_device(): outer = lax.ppermute(outer, 'region', pairs['outer'])]
    pallas_call x1, Pallas kernels: 0.77 us -> 3.32 us  [pack(): pl.pallas_call(functools.partial(pack_kernel, half), grid=(1,), out_shape...]
    ppermute x6, waiting for transfers between devices: 1.27 us -> 2.88 us  [the longest x1 2.87 us: per_device(): outer = lax.ppermute(outer, 'region', pairs['outer'])]
    pallas_call x1, Pallas kernels: 15.6 us -> 16.5 us  [main(): pl.pallas_call(functools.partial(main_kernel, half), grid=(count,), out_s...]
    another operation x0 -> x1, other arithmetic: none -> 0.56 us  [per_device(): jnp.stack([lax.axis_index('region') % 2, lax.axis_index('band') % 2])]
where the time goes in v1:
time: 50.4 us; the launch traced here: 50.1 us
  Pallas kernels  21.5 us (43%)
  blocking collectives  11.9 us (24%)
  starting transfers between devices  10.8 us (21%)
  waiting for transfers between devices  2.88 us (6%)
  local copies, waits for them, and re-layouts  1.61 us (3%)
  between operations  0.76 us (2%)
  other arithmetic  0.62 us (1%)
    pallas_call x1, Pallas kernels, main(): pl.pallas_call(functools.partial(main_kernel, half), grid=(count,), out_s...  16.5 us
    all_to_all x1, blocking collectives, per_device(): shares = lax.all_to_all(quads, ('region', 'band'), 0, 0, tiled=True)  11.9 us
    ppermute x1, starting transfers between devices, per_device(): outer = lax.ppermute(outer, 'region', pairs['outer'])  3.58 us
    pallas_call x1, Pallas kernels, pack(): pl.pallas_call(functools.partial(pack_kernel, half), grid=(1,), out_shape...  3.32 us
    ppermute x1, starting transfers between devices, per_device(): inner = lax.ppermute(inner, 'region', pairs['inner'])  2.96 us
    ppermute x1, starting transfers between devices, per_device(): lax.ppermute(jnp.where(odd[1] != 0, top, bottom), 'band', pairs['near'])  2.95 us
    ppermute x1, waiting for transfers between devices, per_device(): outer = lax.ppermute(outer, 'region', pairs['outer'])  2.87 us
    pallas_call x1, Pallas kernels, tables(): pl.pallas_call(table_kernel, out_shape=(jax.ShapeDtypeStruct((2 * LANES,...  1.75 us
  transfers between devices with their start and end apart: 6, of which 1 were waited for; matrix products, arithmetic and copies ran while one was open for 0% of the time, Pallas kernels for 3%

profile of v1, /device:TPU:0, one launch (start us, length us, event | category | flops | bytes accessed | tf_op | source)
XLA Modules:
  0.0 50.1 jit_solution(7157037934843904859)
XLA Ops:
  0.6 0.6 %pad_add_fusion.odd_ref = s32[2]{0:T(128)} fusion(s32[1]{0:T(128)} %bitcast.1, s32[1]{0:T(128)} %bitcast), kind=kLoop, calls=%fused_computation.4 | loop fusion | flops 2 | bytes 16 | tf_op jit(solution)/shard_map/stack | solution.py:301
  1.2 3.3 %pack.1 = (bf16[2,128,128]{2,1,0:T(8,128)(2,1)}, bf16[2,128,128]{2,1,0:T(8,128)(2,1)}, bf16[4,4,16,1024]{3,2,1,0:T(8,128)(2,1)}, bf16[4,4,16,1024]{3,2,1,0:T(8,128)(2,1)}) custom-call(s32[2]{0:T(128)} %pad_add_fusion.odd_ref, s32[2,1,128]{2,1,0:T(1,128)} %bitcast.7, bf16[4,4,128,1024]{3,2,1,0:T(8,128)(2,1)} %x_ref.1, bf16[4,4,128,1024]{3,2,1,0:T(8,128)(2,1)} %x_ref.1, ...), custom_call_target="tpu_custom_call" | custom-call | tf_op jit(solution)/shard_map/pack/pallas_call | solution.py:76
  4.5 3.0 %collective-permute-start = (bf16[2,128,128]{2,1,0:T(8,128)(2,1)}, bf16[2,128,128]{2,1,0:T(8,128)(2,1)S(1)}, u32[]{:S(2)}, u32[]{:S(2)}) collective-permute-start(bf16[2,128,128]{2,1,0:T(8,128)(2,1)} %get-tuple-element.12), channel_id=1, source_target_pairs={{0,4},{4,0},{8,12},{12,8},{16,20},{20,16},{24,28},{28,24},{1,5},{5... | collective-permute-start | bytes 196616 | tf_op jit(solution)/shard_map/ppermute | solution.py:304
  7.5 3.6 %collective-permute-start.1 = (bf16[2,128,128]{2,1,0:T(8,128)(2,1)}, bf16[2,128,128]{2,1,0:T(8,128)(2,1)S(1)}, u32[]{:S(2)}, u32[]{:S(2)}) collective-permute-start(bf16[2,128,128]{2,1,0:T(8,128)(2,1)} %get-tuple-element.13), channel_id=1, source_target_pairs={{0,28},{4,8},{8,4},{12,16},{16,12},{20,24},{24,20},{28,0},{1,29},{... | collective-permute-start | bytes 196616 | tf_op jit(solution)/shard_map/ppermute | solution.py:305
  11.1 0.0 collective-permute-start.2
  11.1 0.7 %collective-permute-start.3 = (bf16[4,4,16,1024]{3,2,1,0:T(8,128)(2,1)}, bf16[4,4,16,1024]{3,2,1,0:T(8,128)(2,1)S(1)}, u32[]{:S(2)}, u32[]{:S(2)}) collective-permute-start(bf16[4,4,16,1024]{3,2,1,0:T(8,128)(2,1)} %get-tuple-element.15), channel_id=1, source_target_pairs={{1,2},{2,1},{5,6},{6,5},{9,10},{10,9},{13,14},{14,13},{17,18},{18,... | collective-permute-start | bytes 1572872 | tf_op jit(solution)/shard_map/ppermute | solution.py:307
  11.8 0.0 collective-permute-done.inner_ref
  11.8 0.0 copy-start.2
  11.8 2.9 %collective-permute-done.1.outer_ref = bf16[2,128,128]{2,1,0:T(8,128)(2,1)S(1)} collective-permute-done((bf16[2,128,128]{2,1,0:T(8,128)(2,1)}, bf16[2,128,128]{2,1,0:T(8,128)(2,1)S(1)}, u32[]{:S(2)}, u32[]{:S(2)}) %collective-permute-start.1) | collective-permute-done | bytes 65568 | tf_op jit(solution)/shard_map/ppermute | solution.py:305
  14.7 0.0 copy-start.3
  14.7 0.7 %collective-permute-start.5 = (bf16[4,16,128]{2,1,0:T(8,128)(2,1)S(1)}, bf16[4,16,128]{2,1,0:T(8,128)(2,1)S(1)}, u32[]{:S(2)}, u32[]{:S(2)}) collective-permute-start(bf16[4,16,128]{2,1,0:T(8,128)(2,1)S(1)} %get-tuple-element.22), channel_id=1, source_target_pairs={{1,2},{2,1},{5,6},{6,5},{9,10},{10,9},{13,14},{14,13},{17,18},{18,... | collective-permute-start | bytes 49160 | tf_op jit(solution)/shard_map/ppermute | solution.py:312
  15.4 2.9 %collective-permute-start.4 = (bf16[4,16,128]{2,1,0:T(8,128)(2,1)S(1)}, bf16[4,16,128]{2,1,0:T(8,128)(2,1)S(1)}, u32[]{:S(2)}, u32[]{:S(2)}) collective-permute-start(bf16[4,16,128]{2,1,0:T(8,128)(2,1)S(1)} %get-tuple-element.23), channel_id=1, source_target_pairs={{0,1},{1,0},{2,3},{3,2},{4,5},{5,4},{6,7},{7,6},{8,9},{9,8},{10,11... | collective-permute-start | bytes 49160 | tf_op jit(solution)/shard_map/ppermute | solution.py:311
  18.3 1.7 %tables.1 = (bf16[256,256]{1,0:T(8,128)(2,1)}, bf16[2,128,160]{2,1,0:T(8,128)(2,1)}) custom-call(f32[2,2,17]{2,1,0:T(2,128)} %taps_ref.1), custom_call_target="tpu_custom_call" | custom-call | tf_op jit(solution)/shard_map/tables/pallas_call | solution.py:115
  20.0 0.0 collective-permute-done.5.far_corner_ref
  20.1 0.0 copy-start.4
  20.1 0.0 collective-permute-done.4.near_corner_ref
  20.1 0.0 copy-start.5
  20.1 0.0 collective-permute-done.2.near_ref
  20.1 0.0 copy-start
  20.1 0.0 collective-permute-done.3.far_ref
  20.1 0.0 copy-start.1
  20.1 0.0 copy-done.2
  20.1 0.0 copy-done.3
  20.1 0.5 %copy-done.4 = bf16[4,16,128]{2,1,0:T(8,128)(2,1)} copy-done((bf16[4,16,128]{2,1,0:T(8,128)(2,1)}, bf16[4,16,128]{2,1,0:T(8,128)(2,1)S(1)}, u32[]{:S(2)}) %copy-start.4) | copy-done | bytes 16408
  20.7 0.0 copy-done.5
  20.7 0.2 copy-done
  20.9 0.2 copy-done.1
  21.1 16.5 %covariance.1 = (bf16[4,4,128,1024]{3,2,1,0:T(8,128)(2,1)}, f32[32,128]{1,0:T(8,128)}) custom-call(s32[2]{0:T(128)} %pad_add_fusion.odd_ref, f32[2,4,4]{2,1,0:T(4,128)} %mixing_ref.1, f32[4]{0:T(128)} %nugget_ref.1, s32[2,1,128]{2,1,0:T(1,128)} %bitcast.8, bf16[256,256]{1,0:T(8,128)(2,1)} %get-tuple-element.10.across_ref, ...), custom_call_target="tpu_custom_call" | custom-call | tf_op jit(solution)/shard_map/covariance/pallas_call | solution.py:258
  37.5 11.9 %all_to_all.9 = f32[32,1,128]{2,1,0:T(1,128)S(1)} all-to-all(f32[32,1,128]{2,1,0:T(1,128)} %bitcast.6), channel_id=1, replica_groups=mesh['region'=8,'band'=4] {'region','band'}, dimensions={0} | all-to-all | bytes 32768 | tf_op jit(solution)/shard_map/all_to_all | solution.py:330
  49.4 0.1 reduce_sum.9
  49.4 0.7 %div.6 = f32[4,3]{1,0:T(4,128)} reshape(f32[12]{0:T(128)S(1)} %slice_multiply_fusion) | data formatting | bytes 96 | tf_op jit(solution)/shard_map/div | solution.py:332
  (4 shorter events, 0.0 us)
Async XLA Ops:
  4.5 7.2 %collective-permute-start = (bf16[2,128,128]{2,1,0:T(8,128)(2,1)}, bf16[2,128,128]{2,1,0:T(8,128)(2,1)S(1)}, u32[]{:S(2)}, u32[]{:S(2)}) collective-permute-start(bf16[2,128,128]{2,1,0:T(8,128)(2,1)} %get-tuple-element.12), channel_id=1, source_target_pairs={{0,4},{4,0},{8,12},{12,8},{16,20},{20,16},{24,28},{28,24},{1,5},{5... | collective-permute-start | bytes 196616 | tf_op jit(solution)/shard_map/ppermute | solution.py:304
  7.5 7.2 %collective-permute-start.1 = (bf16[2,128,128]{2,1,0:T(8,128)(2,1)}, bf16[2,128,128]{2,1,0:T(8,128)(2,1)S(1)}, u32[]{:S(2)}, u32[]{:S(2)}) collective-permute-start(bf16[2,128,128]{2,1,0:T(8,128)(2,1)} %get-tuple-element.13), channel_id=1, source_target_pairs={{0,28},{4,8},{8,4},{12,16},{16,12},{20,24},{24,20},{28,0},{1,29},{... | collective-permute-start | bytes 196616 | tf_op jit(solution)/shard_map/ppermute | solution.py:305
  11.1 9.0 %collective-permute-start.2 = (bf16[4,4,16,1024]{3,2,1,0:T(8,128)(2,1)}, bf16[4,4,16,1024]{3,2,1,0:T(8,128)(2,1)S(1)}, u32[]{:S(2)}, u32[]{:S(2)}) collective-permute-start(bf16[4,4,16,1024]{3,2,1,0:T(8,128)(2,1)} %get-tuple-element.14), channel_id=1, source_target_pairs={{0,1},{1,0},{2,3},{3,2},{4,5},{5,4},{6,7},{7,6},{8,9},{9,8},{10,11... | collective-permute-start | bytes 1572872 | tf_op jit(solution)/shard_map/ppermute | solution.py:306
  11.1 9.0 %collective-permute-start.3 = (bf16[4,4,16,1024]{3,2,1,0:T(8,128)(2,1)}, bf16[4,4,16,1024]{3,2,1,0:T(8,128)(2,1)S(1)}, u32[]{:S(2)}, u32[]{:S(2)}) collective-permute-start(bf16[4,4,16,1024]{3,2,1,0:T(8,128)(2,1)} %get-tuple-element.15), channel_id=1, source_target_pairs={{1,2},{2,1},{5,6},{6,5},{9,10},{10,9},{13,14},{14,13},{17,18},{18,... | collective-permute-start | bytes 1572872 | tf_op jit(solution)/shard_map/ppermute | solution.py:307
  11.8 8.3 %copy-start.2 = (bf16[2,128,128]{2,1,0:T(8,128)(2,1)}, bf16[2,128,128]{2,1,0:T(8,128)(2,1)S(1)}, u32[]{:S(2)}) copy-start(bf16[2,128,128]{2,1,0:T(8,128)(2,1)S(1)} %collective-permute-done.inner_ref) | copy-start | bytes 196612
  14.7 5.5 %copy-start.3 = (bf16[2,128,128]{2,1,0:T(8,128)(2,1)}, bf16[2,128,128]{2,1,0:T(8,128)(2,1)S(1)}, u32[]{:S(2)}) copy-start(bf16[2,128,128]{2,1,0:T(8,128)(2,1)S(1)} %collective-permute-done.1.outer_ref) | copy-start | bytes 196612
  14.7 5.4 %collective-permute-start.5 = (bf16[4,16,128]{2,1,0:T(8,128)(2,1)S(1)}, bf16[4,16,128]{2,1,0:T(8,128)(2,1)S(1)}, u32[]{:S(2)}, u32[]{:S(2)}) collective-permute-start(bf16[4,16,128]{2,1,0:T(8,128)(2,1)S(1)} %get-tuple-element.22), channel_id=1, source_target_pairs={{1,2},{2,1},{5,6},{6,5},{9,10},{10,9},{13,14},{14,13},{17,18},{18,... | collective-permute-start | bytes 49160 | tf_op jit(solution)/shard_map/ppermute | solution.py:312
  15.4 4.7 %collective-permute-start.4 = (bf16[4,16,128]{2,1,0:T(8,128)(2,1)S(1)}, bf16[4,16,128]{2,1,0:T(8,128)(2,1)S(1)}, u32[]{:S(2)}, u32[]{:S(2)}) collective-permute-start(bf16[4,16,128]{2,1,0:T(8,128)(2,1)S(1)} %get-tuple-element.23), channel_id=1, source_target_pairs={{0,1},{1,0},{2,3},{3,2},{4,5},{5,4},{6,7},{7,6},{8,9},{9,8},{10,11... | collective-permute-start | bytes 49160 | tf_op jit(solution)/shard_map/ppermute | solution.py:311
  20.1 0.6 %copy-start.4 = (bf16[4,16,128]{2,1,0:T(8,128)(2,1)}, bf16[4,16,128]{2,1,0:T(8,128)(2,1)S(1)}, u32[]{:S(2)}) copy-start(bf16[4,16,128]{2,1,0:T(8,128)(2,1)S(1)} %collective-permute-done.5.far_corner_ref) | copy-start | bytes 49156
  20.1 0.6 %copy-start.5 = (bf16[4,16,128]{2,1,0:T(8,128)(2,1)}, bf16[4,16,128]{2,1,0:T(8,128)(2,1)S(1)}, u32[]{:S(2)}) copy-start(bf16[4,16,128]{2,1,0:T(8,128)(2,1)S(1)} %collective-permute-done.4.near_corner_ref) | copy-start | bytes 49156
  20.1 0.8 %copy-start = (bf16[4,4,16,1024]{3,2,1,0:T(8,128)(2,1)}, bf16[4,4,16,1024]{3,2,1,0:T(8,128)(2,1)S(1)}, u32[]{:S(2)}) copy-start(bf16[4,4,16,1024]{3,2,1,0:T(8,128)(2,1)S(1)} %collective-permute-done.2.near_ref) | copy-start | bytes 1572868
  20.1 1.0 %copy-start.1 = (bf16[4,4,16,1024]{3,2,1,0:T(8,128)(2,1)}, bf16[4,4,16,1024]{3,2,1,0:T(8,128)(2,1)S(1)}, u32[]{:S(2)}) copy-start(bf16[4,4,16,1024]{3,2,1,0:T(8,128)(2,1)S(1)} %collective-permute-done.3.far_ref) | copy-start | bytes 1572868

commit v2 on v0

v2 whole, which is shorter than its diff:
```python
import functools

import jax
import jax.numpy as jnp
from jax import lax
from jax.experimental import pallas as pl
from jax.experimental.pallas import tpu as pltpu
from jax.sharding import PartitionSpec as P

LANES = 128
BF16 = jnp.bfloat16
F32 = jnp.float32
SMEM = pl.BlockSpec(memory_space=pltpu.SMEM)


def lanes_of(tile):
    return slice(tile * LANES, (tile + 1) * LANES)


def whole(a):
    return pl.BlockSpec(a.shape, lambda *_: (0,) * len(a.shape))


def odd(axis):
    return lax.axis_index(axis) % 2 != 0


def bounds_by_row(span_ref):
    return [jnp.broadcast_to(span_ref[entry].astype(F32), (LANES, LANES)).T for entry in range(2)]


def land_tile(low, high, first_col):
    column = (lax.broadcasted_iota(jnp.int32, low.shape, 1) + first_col).astype(F32)
    return ((column >= low) & (column < high)).astype(F32).astype(BF16)


def pack_kernel(half, cols, span_ref, west_ref, east_ref, inner_ref, outer_ref):
    probes, variables, _, _ = west_ref.shape
    per_group = LANES // half
    low, high = bounds_by_row(span_ref)
    first = land_tile(low, high, 0)
    last = land_tile(low, high, cols - LANES)
    swapped = odd("region")
    for group in range(inner_ref.shape[0]):
        heads, tails = [], []
        for plane in range(group * per_group, (group + 1) * per_group):
            at = (plane // variables, plane % variables)
            heads.append((west_ref[at] * first)[:, :half])
            tails.append((east_ref[at] * last)[:, LANES - half :])
        left, right = jnp.concatenate(heads, axis=1), jnp.concatenate(tails, axis=1)
        inner_ref[group] = jnp.where(swapped, left, right)
        outer_ref[group] = jnp.where(swapped, right, left)


def pack(probes, span, half):
    count, variables, rows, cols = probes.shape
    edge = jax.ShapeDtypeStruct((count * variables * half // LANES, rows, LANES), BF16)
    tile = lambda at: pl.BlockSpec((count, variables, rows, LANES), lambda _: (0, 0, 0, at))
    kernel = functools.partial(pack_kernel, half, cols)
    return pl.pallas_call(
        kernel,
        grid=(1,),
        out_shape=(edge, edge),
        in_specs=[whole(span), tile(0), tile(cols // LANES - 1)],
        out_specs=(whole(edge), whole(edge)),
        compiler_params=pltpu.CompilerParams(vmem_limit_bytes=16 << 20),
        name="pack",
    )(span, probes, probes)


def prepare_kernel(
    half,
    taps_ref,
    mixing_ref,
    span_ref,
    top_ref,
    bottom_ref,
    near_ref,
    far_ref,
    shore_ref,
    across_ref,
    downward_ref,
    fringe_ref,
):
    probes, variables, _, cols = top_ref.shape
    kernels = downward_ref.shape[0]
    swapped = odd("band")
    low, high = bounds_by_row(span_ref)
    for tile in range(cols // LANES):
        lanes = lanes_of(tile)
        above = land_tile(low[:half], high[:half], tile * LANES)
        below = land_tile(low[-half:], high[-half:], tile * LANES)
        shore_ref[0, :, lanes] = above
        shore_ref[1, :, lanes] = below
        for plane in range(probes * variables):
            at = (plane // variables, plane % variables, slice(None), lanes)
            up, down = top_ref[at] * above, bottom_ref[at] * below
            near_ref[plane, :, lanes] = jnp.where(swapped, up, down)
            far_ref[plane, :, lanes] = jnp.where(swapped, down, up)

    def filtered(kernel, which, distance):
        table = jnp.zeros(distance.shape, F32)
        for tap in range(half + 1):
            table = jnp.where(distance == tap, taps_ref[kernel, which, tap], table)
        return table.astype(BF16)

    def places(shape):
        return lax.broadcasted_iota(jnp.int32, shape, 0), lax.broadcasted_iota(jnp.int32, shape, 1)

    for kernel in range(kernels):
        row, column = places((across_ref.shape[0], LANES))
        across_ref[:, lanes_of(kernel)] = filtered(kernel, 0, jnp.abs(row - column - half))
        row, column = places(downward_ref.shape[1:])
        downward_ref[kernel] = filtered(kernel, 1, jnp.abs(row - column))
        size = fringe_ref.shape[1]
        row, column = places((size, size))
        bits = half.bit_length() - 1
        i, h = row & (half - 1), column & (half - 1)
        side = (row >> bits) & 1
        gap = jnp.where(side == 0, i - h, h - i)
        reach = (gap <= 0) & (side == ((column >> bits) & 1))
        weight = filtered(kernel, 1, jnp.where(reach, gap + half, -1)).astype(F32)
        v, w = row >> (bits + 1), column >> (bits + 1)
        mixed = jnp.zeros((size, size), F32)
        for a in range(variables):
            for b in range(variables):
                mixed = jnp.where((v == a) & (w == b), mixing_ref[kernel, a, b], mixed)
        weight = weight * mixed
        coarse = weight.astype(BF16)
        fringe_ref[kernel, :, :size] = coarse
        fringe_ref[kernel, :, size:] = (weight - coarse.astype(F32)).astype(BF16)


def prepare(probes, taps, mixing, span, half):
    count, variables, rows, cols = probes.shape
    kernels = taps.shape[0]
    size = 2 * half * variables
    strip = jax.ShapeDtypeStruct((count * variables + 1, half, cols), BF16)
    outs = (
        strip,
        strip,
        jax.ShapeDtypeStruct((2, half, cols), BF16),
        jax.ShapeDtypeStruct((2 * LANES, kernels * LANES), BF16),
        jax.ShapeDtypeStruct((kernels, rows, rows), BF16),
        jax.ShapeDtypeStruct((kernels, size, 2 * size), BF16),
    )
    edge = lambda at: pl.BlockSpec((count, variables, half, cols), lambda _: (0, 0, at, 0))
    return pl.pallas_call(
        functools.partial(prepare_kernel, half),
        grid=(1,),
        out_shape=outs,
        in_specs=[SMEM, SMEM, whole(span), edge(0), edge(rows // half - 1)],
        out_specs=tuple(whole(o) for o in outs),
        cost_estimate=pl.CostEstimate(flops=10**7, bytes_accessed=4 << 20, transcendentals=0),
        compiler_params=pltpu.CompilerParams(vmem_limit_bytes=16 << 20),
        name="prepare",
    )(taps, mixing, span, probes, probes)


def corner_kernel(inner_ref, outer_ref, near_in, far_in, near_ref, far_ref):
    half = near_ref.shape[1]
    groups, rows, _ = inner_ref.shape
    swapped = odd("band")
    for at, ref in ((0, inner_ref), (groups, outer_ref)):
        for group in range(groups):
            up, down = ref[group, :half], ref[group, rows - half :]
            near_ref[0, :, lanes_of(at + group)] = jnp.where(swapped, up, down)
            far_ref[0, :, lanes_of(at + group)] = jnp.where(swapped, down, up)
    rest = slice(2 * groups * LANES, near_ref.shape[2])
    near_ref[0, :, rest] = jnp.zeros_like(near_ref[0, :, rest])
    far_ref[0, :, rest] = jnp.zeros_like(far_ref[0, :, rest])


def corner(inner, outer, near, far):
    last = pl.BlockSpec((1, *near.shape[1:]), lambda _: (near.shape[0] - 1, 0, 0))
    keep = pl.BlockSpec(memory_space=pl.ANY)
    return pl.pallas_call(
        corner_kernel,
        grid=(1,),
        out_shape=(jax.ShapeDtypeStruct(near.shape, BF16),) * 2,
        in_specs=[whole(inner), whole(outer), keep, keep],
        out_specs=(last, last),
        input_output_aliases={2: 0, 3: 1},
        compiler_params=pltpu.CompilerParams(vmem_limit_bytes=16 << 20),
        name="corner",
    )(inner, outer, near, far)


def side(block, probe, half, variables):
    per_group = LANES // half // variables
    return pltpu.roll(block.astype(F32), (per_group - probe % per_group) * (half * variables) % LANES, 1)


def extend(put, height, half, variables, tiles, tile_of, west, east):
    lane = lax.broadcasted_iota(jnp.int32, (height, LANES), 1)
    for v in range(variables):
        back = LANES - half * v
        before = pltpu.roll(west, back % LANES, 1)
        for tile in range(tiles):
            moved = pltpu.roll(tile_of(v, tile).astype(F32), half, 1)
            put(v, tile, jnp.where(lane < half, before, moved).astype(BF16))
            before = moved
        after = pltpu.roll(east, (back + half) % LANES, 1)
        final = jnp.where(lane < half, before, jnp.where(lane < 2 * half, after, 0.0))
        put(v, tiles, final.astype(BF16))


def fold(part):
    height, width = part.shape
    folded = jnp.sum(part.reshape(height // 8, 8, width), axis=0)
    return sum(folded[:, lanes_of(t)] for t in range(width // LANES))


def own_kernel(
    half,
    mixing_ref,
    nugget_ref,
    span_ref,
    across_ref,
    downward_ref,
    x_ref,
    inner_ref,
    outer_ref,
    out_ref,
    edge_ref,
    sums_ref,
    land_ref,
    ext_ref,
    interior_ref,
):
    probe = pl.program_id(0)
    variables, rows, cols = x_ref.shape[1:]
    kernels = downward_ref.shape[0]
    tiles = cols // LANES

    @pl.when(probe == 0)
    def _():
        low, high = bounds_by_row(span_ref)
        for tile in range(tiles):
            land_ref[:, lanes_of(tile)] = land_tile(low, high, tile * LANES)

    group = probe // (LANES // half // variables)
    swapped = odd("region")
    inner, outer = inner_ref[group], outer_ref[group]

    def put(v, tile, value):
        ext_ref[v, :, lanes_of(tile)] = value

    extend(
        put,
        rows,
        half,
        variables,
        tiles,
        lambda v, t: x_ref[0, v, :, lanes_of(t)] * land_ref[:, lanes_of(t)],
        side(jnp.where(swapped, inner, outer), probe, half, variables),
        side(jnp.where(swapped, outer, inner), probe, half, variables),
    )
    for tile in range(tiles):
        window = ext_ref[:, :, tile * LANES : (tile + 2) * LANES].reshape(variables * rows, 2 * LANES)
        both = jnp.dot(window, across_ref[...], preferred_element_type=F32).astype(BF16)
        for kernel in range(kernels):
            interior_ref[kernel, :, :, lanes_of(tile)] = both[:, lanes_of(kernel)].reshape(variables, rows, LANES)

    sums = [jnp.zeros((8, LANES), F32) for _ in range(kernels + 1)]
    wide = 2 * LANES
    for chunk in range(cols // wide):
        span = slice(chunk * wide, (chunk + 1) * wide)
        smooth = [
            [
                jnp.dot(downward_ref[kernel], interior_ref[kernel, w, :, span], preferred_element_type=F32)
                for w in range(variables)
            ]
            for kernel in range(kernels)
        ]
        land = land_ref[:, span].astype(F32)
        for v in range(variables):
            local = (x_ref[0, v, :, span] * land_ref[:, span]).astype(F32)
            total = nugget_ref[v] * local
            parts = [total * local]
            for kernel in range(kernels):
                term = mixing_ref[kernel, v, 0] * smooth[kernel][0]
                for w in range(1, variables):
                    term = term + mixing_ref[kernel, v, w] * smooth[kernel][w]
                parts.append(term * local)
                total = total + term
            out_ref[0, v, :, span] = (total * land).astype(BF16)
            edge_ref[0, v, 0, :, span] = total[:half]
            edge_ref[0, v, 1, :, span] = total[rows - half :]
            for k, part in enumerate(parts[1:] + parts[:1]):
                sums[k] = sums[k] + fold(part)
    for k in range(kernels + 1):
        sums_ref[0, k] = sums[k]


def own(mixing, nugget, span, across, downward, probes, inner, outer, half):
    count, variables, rows, cols = probes.shape
    kernels = downward.shape[0]
    block = lambda *shape: pl.BlockSpec((1, *shape), lambda p: (p,) + (0,) * len(shape))
    outs = (
        jax.ShapeDtypeStruct(probes.shape, BF16),
        jax.ShapeDtypeStruct((count, variables, 2, half, cols), F32),
        jax.ShapeDtypeStruct((count, kernels + 1, 8, LANES), F32),
    )
    return pl.pallas_call(
        functools.partial(own_kernel, half),
        grid=(count,),
        out_shape=outs,
        in_specs=[
            SMEM,
            SMEM,
            whole(span),
            whole(across),
            whole(downward),
            block(*probes.shape[1:]),
            whole(inner),
            whole(outer),
        ],
        out_specs=tuple(block(*o.shape[1:]) for o in outs),
        scratch_shapes=[
            pltpu.VMEM((rows, cols), BF16),
            pltpu.VMEM((variables, rows, cols + LANES), BF16),
            pltpu.VMEM((kernels, variables, rows, cols), BF16),
        ],
        cost_estimate=pl.CostEstimate(flops=10**10, bytes_accessed=16 << 20, transcendentals=0),
        compiler_params=pltpu.CompilerParams(vmem_limit_bytes=32 << 20),
        name="own",
    )(mixing, nugget, span, across, downward, probes, inner, outer)


def border_kernel(
    half,
    across_ref,
    fringe_ref,
    shore_ref,
    near_ref,
    far_ref,
    near_corner_ref,
    far_corner_ref,
    near_own_ref,
    far_own_ref,
    edge_ref,
    sums_ref,
    base_ref,
    out_ref,
    quad_ref,
    ext_ref,
    ready_ref,
    total_ref,
    sem,
):
    probe = pl.program_id(0)
    variables, _, cols = near_ref.shape
    rows = out_ref.shape[2]
    count, shares = sums_ref.shape[:2]
    kernels = shares - 1
    tiles = cols // LANES
    group = probe // (LANES // half // variables)
    groups = count * variables * half // LANES
    swapped, flipped = odd("band"), odd("region")
    size = 2 * half * variables

    for at in range(2):
        from_near = swapped if at == 0 else jnp.logical_not(swapped)
        corners = []
        for kind in (0, groups):
            where = pl.ds(pl.multiple_of((kind + group) * LANES, LANES), LANES)
            corners.append(jnp.where(from_near, near_corner_ref[0, :, where], far_corner_ref[0, :, where]))
        inner, outer = corners

        def put(v, tile, value, at=at):
            first = (2 * v + at) * half
            ext_ref[first : first + half, lanes_of(tile)] = value

        extend(
            put,
            half,
            half,
            variables,
            tiles,
            lambda v, t, n=from_near: jnp.where(n, near_ref[v, :, lanes_of(t)], far_ref[v, :, lanes_of(t)]),
            side(jnp.where(flipped, inner, outer), probe, half, variables),
            side(jnp.where(flipped, outer, inner), probe, half, variables),
        )

    for tile in range(tiles):
        both = jnp.dot(
            ext_ref[:, tile * LANES : (tile + 2) * LANES], across_ref[...], preferred_element_type=F32
        ).astype(BF16)
        for kernel in range(kernels):
            piece = both[:, lanes_of(kernel)]
            ready_ref[kernel, :size, lanes_of(tile)] = piece
            ready_ref[kernel, size:, lanes_of(tile)] = piece

    sums = [sums_ref[probe, k] for k in range(shares)]
    wide = 2 * LANES
    for chunk in range(cols // wide):
        span = slice(chunk * wide, (chunk + 1) * wide)
        up = jnp.where(swapped, near_own_ref[:, :, span], far_own_ref[:, :, span])
        down = jnp.where(swapped, far_own_ref[:, :, span], near_own_ref[:, :, span])
        total = edge_ref[0, :, :, :, span]
        local = jnp.concatenate([up[:, None], down[:, None]], axis=1).astype(F32)
        for kernel in range(kernels):
            term = jnp.dot(fringe_ref[kernel], ready_ref[kernel, :, span], preferred_element_type=F32)
            sums[kernel] = sums[kernel] + fold(term * local.reshape(size, wide))
            total = total + term.reshape(total.shape)
        total_ref[probe, :, :, :, span] = (total * shore_ref[:, :, span].astype(F32)[None]).astype(BF16)

    def copies(p):
        for at, first in ((0, 0), (1, rows - half)):
            yield pltpu.make_async_copy(
                total_ref.at[p, :, at], out_ref.at[p, :, pl.ds(first, half), :], sem.at[p, at]
            )

    for copy in copies(probe):
        copy.start()

    lane = lax.broadcasted_iota(jnp.int32, quad_ref.shape, 1)
    line = jnp.where(probe == 0, 0.0, quad_ref[...])
    for k in range(shares):
        line = jnp.where(lane == probe * shares + k, jnp.sum(sums[k]), line)
    quad_ref[...] = line

    @pl.when(probe == count - 1)
    def _():
        for p in range(count):
            for copy in copies(p):
                copy.wait()


def border(across, fringe, shore, near, far, near_own, far_own, edge, sums, base, half, devices):
    count, variables, rows, cols = base.shape
    kernels = fringe.shape[0]
    size = 2 * half * variables
    planes = pl.BlockSpec((variables, half, cols), lambda p: (p, 0, 0))
    last = pl.BlockSpec((1, half, cols), lambda p: (count * variables, 0, 0))
    keep = pl.BlockSpec(memory_space=pl.ANY)
    return pl.pallas_call(
        functools.partial(border_kernel, half),
        grid=(count,),
        out_shape=(jax.ShapeDtypeStruct(base.shape, BF16), jax.ShapeDtypeStruct((devices, LANES), F32)),
        in_specs=[
            whole(across),
            whole(fringe),
            whole(shore),
            planes,
            planes,
            last,
            last,
            planes,
            planes,
            pl.BlockSpec((1, variables, 2, half, cols), lambda p: (p, 0, 0, 0, 0)),
            whole(sums),
            keep,
        ],
        out_specs=(keep, pl.BlockSpec((devices, LANES), lambda p: (0, 0))),
        scratch_shapes=[
            pltpu.VMEM((size, cols + LANES), BF16),
            pltpu.VMEM((kernels, 2 * size, cols), BF16),
            pltpu.VMEM((count, variables, 2, half, cols), BF16),
            pltpu.SemaphoreType.DMA((count, 2)),
        ],
        input_output_aliases={11: 0},
        compiler_params=pltpu.CompilerParams(vmem_limit_bytes=32 << 20),
        name="border",
    )(across, fringe, shore, near, far, near, far, near_own, far_own, edge, sums, base)


def per_device(probes, filter_taps, mixing, nugget, land_span):
    count, variables, rows, cols = probes.shape
    kernels = filter_taps.shape[0]
    half = filter_taps.shape[2] - 1
    regions, bands = lax.axis_size("region"), lax.axis_size("band")
    inner_pairs = [(i, i ^ 1) for i in range(regions)]
    outer_pairs = [(i, (i + 1 if i % 2 else i - 1) % regions) for i in range(regions)]
    near_pairs = [(i, i ^ 1) for i in range(bands)]
    far_pairs = [(i, i + 1 if i % 2 else i - 1) for i in range(1, bands - 1)]

    probes = pltpu.with_memory_space_constraint(probes, pltpu.HBM)
    span = land_span.reshape(2, 1, rows)
    inner, outer = pack(probes, span, half)
    inner = lax.ppermute(inner, "region", inner_pairs)
    outer = lax.ppermute(outer, "region", outer_pairs)
    near, far, shore, across, downward, fringe = prepare(probes, filter_taps, mixing, span, half)
    near, far = corner(inner, outer, near, far)
    near_halo = lax.ppermute(near, "band", near_pairs)
    far_halo = lax.ppermute(far, "band", far_pairs)
    base, edge, sums = own(mixing, nugget, span, across, downward, probes, inner, outer, half)
    output, quads = border(
        across, fringe, shore, near_halo, far_halo, near, far, edge, sums, base, half, regions * bands
    )
    shares = lax.all_to_all(quads, ("region", "band"), 0, 0, tiled=True)
    quadratic = jnp.sum(shares, axis=0)[: count * (kernels + 1)].reshape(count, kernels + 1)
    return output, quadratic / (bands * rows * cols)


def solution(mesh):
    in_specs = (P(None, None, "band", "region"), P(), P(), P(), P(None, "band", "region"))
    out_specs = (P(None, None, "band", "region"), P())
    return jax.shard_map(
        per_device, mesh=mesh, in_specs=in_specs, out_specs=out_specs, check_vma=False
    )
```

time: 54.4 us -> 47.9 us (0.88)
  starting transfers between devices: 14.9 us -> 7.37 us
  local copies, waits for them, and re-layouts: 7.53 us -> 1.35 us
  Pallas kernels: 18.1 us -> 23.6 us
  blocking collectives: 11.4 us -> 13.7 us
    ppermute x6 -> x4, starting transfers between devices: 14.9 us -> 7.37 us  [the longest x1 3.57 us: per_device(): outer = lax.ppermute(outer, 'region', outer_pairs)]
    unnamed x16 -> x10, local copies, waits for them, and re-layouts: 6.86 us -> 0.69 us
    pallas_call x3 -> x5, Pallas kernels: 18.1 us -> 23.6 us  [the longest x1 15.3 us: own(): pl.pallas_call(functools.partial(own_kernel, half), grid=(count,), out_sh...]
    all_to_all x1, blocking collectives: 11.4 us -> 13.7 us  [per_device(): shares = lax.all_to_all(quads, ('region', 'band'), 0, 0, tiled=True)]
    ppermute x6 -> x4, waiting for transfers between devices: 1.27 us -> 0.9 us  [the longest x1 0.89 us: per_device(): outer = lax.ppermute(outer, 'region', outer_pairs)]
  transfers between devices with their start and end apart: 6 -> 4, of which waited for: 1 -> 1; matrix products, arithmetic and copies ran while one was open for 0% -> 0% of each run, Pallas kernels for 3% -> 37%
where the time goes in v2:
time: 47.9 us; the launch traced here: 47.6 us
  Pallas kernels  23.6 us (49%)
  blocking collectives  13.7 us (29%)
  starting transfers between devices  7.37 us (15%)
  local copies, waits for them, and re-layouts  1.35 us (3%)
  waiting for transfers between devices  0.9 us (2%)
  between operations  0.71 us (1%)
    pallas_call x1, Pallas kernels, own(): pl.pallas_call(functools.partial(own_kernel, half), grid=(count,), out_sh...  15.3 us
    all_to_all x1, blocking collectives, per_device(): shares = lax.all_to_all(quads, ('region', 'band'), 0, 0, tiled=True)  13.7 us
    pallas_call x1, Pallas kernels, border(): pl.pallas_call(functools.partial(border_kernel, half), grid=(count,), out...  4.19 us
    ppermute x1, starting transfers between devices, per_device(): outer = lax.ppermute(outer, 'region', outer_pairs)  3.57 us
    ppermute x1, starting transfers between devices, per_device(): inner = lax.ppermute(inner, 'region', inner_pairs)  3.03 us
    pallas_call x1, Pallas kernels, prepare(): pl.pallas_call(functools.partial(prepare_kernel, half), grid=(1,), out_sh...  2.47 us
    pallas_call x1, Pallas kernels, pack(): pl.pallas_call(kernel, grid=(1,), out_shape=(edge, edge), in_specs=[whole...  1.65 us
  transfers between devices with their start and end apart: 4, of which 1 were waited for; matrix products, arithmetic and copies ran while one was open for 0% of the time, Pallas kernels for 37%

profile of v2, /device:TPU:0, one launch (start us, length us, event | category | flops | bytes accessed | tf_op | source)
XLA Modules:
  0.0 47.6 jit_solution(5629379331039579159)
XLA Ops:
  0.6 0.0 copy-start.1
  0.6 0.7 %copy-done.1 = s32[2,128,1]{1,2,0:T(1,128)S(1)} copy-done((s32[2,128,1]{1,2,0:T(1,128)S(1)}, s32[2,128,1]{1,2,0:T(1,128)}, u32[]{:S(2)}) %copy-start.1) | copy-done | bytes 1048
  1.3 0.0 copy-start
  1.3 0.0 copy-start.2
  1.3 0.0 copy-start.3
  1.3 1.6 %pack.1 = (bf16[2,128,128]{2,1,0:T(8,128)(2,1)S(1)}, bf16[2,128,128]{2,1,0:T(8,128)(2,1)S(1)}) custom-call(s32[2,1,128]{2,1,0:T(1,128)S(1)} %bitcast.5, bf16[4,4,128,1024]{3,2,1,0:T(8,128)(2,1)} %x_ref.1, bf16[4,4,128,1024]{3,2,1,0:T(8,128)(2,1)} %x_ref.1), custom_call_target="tpu_custom_call" | custom-call | tf_op jit(solution)/shard_map/pack/pallas_call | solution.py:60
  3.0 3.0 %collective-permute-start = (bf16[2,128,128]{2,1,0:T(8,128)(2,1)S(1)}, bf16[2,128,128]{2,1,0:T(8,128)(2,1)S(1)}, u32[]{:S(2)}, u32[]{:S(2)}) collective-permute-start(bf16[2,128,128]{2,1,0:T(8,128)(2,1)S(1)} %get-tuple-element.20), channel_id=1, source_target_pairs={{0,4},{4,0},{8,12},{12,8},{16,20},{20,16},{24,28},{28,24},{1,5},{5... | collective-permute-start | bytes 196616 | tf_op jit(solution)/shard_map/ppermute | solution.py:482
  6.0 0.0 copy-start.4
  6.0 3.6 %collective-permute-start.1 = (bf16[2,128,128]{2,1,0:T(8,128)(2,1)S(1)}, bf16[2,128,128]{2,1,0:T(8,128)(2,1)S(1)}, u32[]{:S(2)}, u32[]{:S(2)}) collective-permute-start(bf16[2,128,128]{2,1,0:T(8,128)(2,1)S(1)} %get-tuple-element.21), channel_id=1, source_target_pairs={{0,28},{4,8},{8,4},{12,16},{16,12},{20,24},{24,20},{28,0},{1,29},{... | collective-permute-start | bytes 196616 | tf_op jit(solution)/shard_map/ppermute | solution.py:483
  9.6 0.0 copy-done
  9.6 0.0 copy-done.2
  9.6 0.0 copy-done.3
  9.6 2.5 %prepare.1 = (bf16[17,16,1024]{2,1,0:T(8,128)(2,1)S(1)}, bf16[17,16,1024]{2,1,0:T(8,128)(2,1)S(1)}, bf16[2,16,1024]{2,1,0:T(8,128)(2,1)S(1)}, bf16[256,256]{1,0:...) custom-call(f32[2,2,17]{2,1,0:T(2,128)S(1)} %copy-done.3, f32[2,4,4]{2,1,0:T(4,128)S(1)} %copy-done, ...), custom_call_target="tpu_custom_call" | custom-call | flops 10000000 | bytes 4194304 | tf_op jit(solution)/shard_map/prepare/pallas_call | solution.py:148
  12.1 0.0 collective-permute-done.inner_ref
  12.1 0.9 %collective-permute-done.1.outer_ref = bf16[2,128,128]{2,1,0:T(8,128)(2,1)S(1)} collective-permute-done((bf16[2,128,128]{2,1,0:T(8,128)(2,1)S(1)}, bf16[2,128,128]{2,1,0:T(8,128)(2,1)S(1)}, u32[]{:S(2)}, u32[]{:S(2)}) %collective-permute-start.1) | collective-permute-done | bytes 65568 | tf_op jit(solution)/shard_map/ppermute | solution.py:483
  13.0 0.1 collective-permute-start.2
  13.1 0.7 %collective-permute-start.3 = (bf16[17,16,1024]{2,1,0:T(8,128)(2,1)S(1)}, bf16[17,16,1024]{2,1,0:T(8,128)(2,1)S(1)}, u32[]{:S(2)}, u32[]{:S(2)}) collective-permute-start(bf16[17,16,1024]{2,1,0:T(8,128)(2,1)S(1)} %get-tuple-element.25.far_own_ref), channel_id=1, source_target_pairs={{1,2},{2,1},{5,6},{6,5},{9,10},{10,9},{13,14},{14,13},{17,18},{18,... | collective-permute-start | bytes 1671176 | tf_op jit(solution)/shard_map/ppermute | solution.py:487
  13.8 0.0 copy-done.4
  13.8 15.3 %own.1 = (bf16[4,4,128,1024]{3,2,1,0:T(8,128)(2,1)}, f32[4,4,2,16,1024]{4,3,2,1,0:T(8,128)S(1)}, f32[4,3,8,128]{3,2,1,0:T(8,128)S(1)}) custom-call(f32[2,4,4]{2,1,0:T(4,128)S(1)} %copy-done, f32[4]{0:T(128)S(1)} %copy-done.4, s32[2,1,128]{2,1,0:T(1,128)S(1)} %bitcast.7, bf16[256,256]{1,0:T(8,128)(2,1)S(1)} %get-tuple-element.17.across_ref, ...), custom_call_target="tpu_custom_call" | custom-call | flops 10000000000 | bytes 16777216 | tf_op jit(solution)/shard_map/own/pallas_call | solution.py:305
  29.0 0.0 collective-permute-done.2.near_ref.near_corner_ref
  29.0 0.0 collective-permute-done.3.far_ref.far_corner_ref
  29.0 4.2 %border.1 = (bf16[4,4,128,1024]{3,2,1,0:T(8,128)(2,1)}, f32[32,128]{1,0:T(8,128)S(1)}) custom-call(bf16[256,256]{1,0:T(8,128)(2,1)S(1)} %get-tuple-element.17.across_ref, bf16[2,128,256]{2,1,0:T(8,128)(2,1)S(1)} %get-tuple-element.18.fringe_ref, bf16[2,16,1024]{2,1,0:T(8,128)(2,1)S(1)} %get-tuple-element.19.shore_ref, ...), custom_call_target="tpu_custom_call", output_to_operand_aliasing={{0}: (11, {})} | custom-call | tf_op jit(solution)/shard_map/border/pallas_call | solution.py:438
  33.2 13.7 %all_to_all.9 = f32[32,1,128]{2,1,0:T(1,128)S(1)} all-to-all(f32[32,1,128]{2,1,0:T(1,128)S(1)} %bitcast.4), channel_id=1, replica_groups=mesh['region'=8,'band'=4] {'region','band'}, dimensions={0} | all-to-all | bytes 32768 | tf_op jit(solution)/shard_map/all_to_all | solution.py:492
  46.9 0.1 reduce_sum.9
  47.0 0.7 %div.6 = f32[4,3]{1,0:T(4,128)} reshape(f32[12]{0:T(128)S(1)} %slice_multiply_fusion) | data formatting | bytes 96 | tf_op jit(solution)/shard_map/div | solution.py:494
  (2 shorter events, 0.0 us)
Async XLA Ops:
  0.6 0.7 %copy-start.1 = (s32[2,128,1]{1,2,0:T(1,128)S(1)}, s32[2,128,1]{1,2,0:T(1,128)}, u32[]{:S(2)}) copy-start(s32[2,128,1]{1,2,0:T(1,128)} %param.9) | copy-start | bytes 3076
  1.3 8.3 %copy-start = (f32[2,4,4]{2,1,0:T(4,128)S(1)}, f32[2,4,4]{2,1,0:T(4,128)}, u32[]{:S(2)}) copy-start(f32[2,4,4]{2,1,0:T(4,128)} %mixing_ref.3) | copy-start | bytes 388
  1.3 8.3 %copy-start.2 = (s32[2,128,1]{1,2,0:T(1,128)S(1)}, s32[2,128,1]{1,2,0:T(1,128)}, u32[]{:S(2)}) copy-start(s32[2,128,1]{1,2,0:T(1,128)} %param.9) | copy-start | bytes 3076
  1.3 8.3 %copy-start.3 = (f32[2,2,17]{2,1,0:T(2,128)S(1)}, f32[2,2,17]{2,1,0:T(2,128)}, u32[]{:S(2)}) copy-start(f32[2,2,17]{2,1,0:T(2,128)} %taps_ref.1) | copy-start | bytes 820
  3.0 9.1 %collective-permute-start = (bf16[2,128,128]{2,1,0:T(8,128)(2,1)S(1)}, bf16[2,128,128]{2,1,0:T(8,128)(2,1)S(1)}, u32[]{:S(2)}, u32[]{:S(2)}) collective-permute-start(bf16[2,128,128]{2,1,0:T(8,128)(2,1)S(1)} %get-tuple-element.20), channel_id=1, source_target_pairs={{0,4},{4,0},{8,12},{12,8},{16,20},{20,16},{24,28},{28,24},{1,5},{5... | collective-permute-start | bytes 196616 | tf_op jit(solution)/shard_map/ppermute | solution.py:482
  6.0 7.8 %copy-start.4 = (f32[4]{0:T(128)S(1)}, f32[4]{0:T(128)}, u32[]{:S(2)}) copy-start(f32[4]{0:T(128)} %nugget_ref.1) | copy-start | bytes 52
  6.0 7.0 %collective-permute-start.1 = (bf16[2,128,128]{2,1,0:T(8,128)(2,1)S(1)}, bf16[2,128,128]{2,1,0:T(8,128)(2,1)S(1)}, u32[]{:S(2)}, u32[]{:S(2)}) collective-permute-start(bf16[2,128,128]{2,1,0:T(8,128)(2,1)S(1)} %get-tuple-element.21), channel_id=1, source_target_pairs={{0,28},{4,8},{8,4},{12,16},{16,12},{20,24},{24,20},{28,0},{1,29},{... | collective-permute-start | bytes 196616 | tf_op jit(solution)/shard_map/ppermute | solution.py:483
  13.0 16.0 %collective-permute-start.2 = (bf16[17,16,1024]{2,1,0:T(8,128)(2,1)S(1)}, bf16[17,16,1024]{2,1,0:T(8,128)(2,1)S(1)}, u32[]{:S(2)}, u32[]{:S(2)}) collective-permute-start(bf16[17,16,1024]{2,1,0:T(8,128)(2,1)S(1)} %get-tuple-element.24.near_own_ref), channel_id=1, source_target_pairs={{0,1},{1,0},{2,3},{3,2},{4,5},{5,4},{6,7},{7,6},{8,9},{9,8},{10,11... | collective-permute-start | bytes 1671176 | tf_op jit(solution)/shard_map/ppermute | solution.py:486
  13.1 16.0 %collective-permute-start.3 = (bf16[17,16,1024]{2,1,0:T(8,128)(2,1)S(1)}, bf16[17,16,1024]{2,1,0:T(8,128)(2,1)S(1)}, u32[]{:S(2)}, u32[]{:S(2)}) collective-permute-start(bf16[17,16,1024]{2,1,0:T(8,128)(2,1)S(1)} %get-tuple-element.25.far_own_ref), channel_id=1, source_target_pairs={{1,2},{2,1},{5,6},{6,5},{9,10},{10,9},{13,14},{14,13},{17,18},{18,... | collective-permute-start | bytes 1671176 | tf_op jit(solution)/shard_map/ppermute | solution.py:487

commit v3 on v2

v3 whole, which is shorter than its diff:
```python
import functools

import jax
import jax.numpy as jnp
from jax import lax
from jax.experimental import pallas as pl
from jax.experimental.pallas import tpu as pltpu
from jax.sharding import PartitionSpec as P

LANES = 128
BF16 = jnp.bfloat16
F32 = jnp.float32
PARTS = 1
SMEM = pl.BlockSpec(memory_space=pltpu.SMEM)


def lanes_of(tile):
    return slice(tile * LANES, (tile + 1) * LANES)


def whole(a):
    return pl.BlockSpec(a.shape, lambda *_: (0,) * len(a.shape))


def odd(axis):
    return lax.axis_index(axis) % 2 != 0


def bounds_by_row(span_ref):
    return [jnp.broadcast_to(span_ref[entry].astype(F32), (LANES, LANES)).T for entry in range(2)]


def land_tile(low, high, first_col):
    column = (lax.broadcasted_iota(jnp.int32, low.shape, 1) + first_col).astype(F32)
    return ((column >= low) & (column < high)).astype(F32).astype(BF16)


def pack_kernel(half, cols, span_ref, west_ref, east_ref, inner_ref, outer_ref):
    probes, variables, _, _ = west_ref.shape
    per_group = LANES // half
    low, high = bounds_by_row(span_ref)
    first = land_tile(low, high, 0)
    last = land_tile(low, high, cols - LANES)
    swapped = odd("region")
    for group in range(inner_ref.shape[0]):
        heads, tails = [], []
        for plane in range(group * per_group, (group + 1) * per_group):
            at = (plane // variables, plane % variables)
            heads.append((west_ref[at] * first)[:, :half])
            tails.append((east_ref[at] * last)[:, LANES - half :])
        left, right = jnp.concatenate(heads, axis=1), jnp.concatenate(tails, axis=1)
        inner_ref[group] = jnp.where(swapped, left, right)
        outer_ref[group] = jnp.where(swapped, right, left)


def pack(probes, span, half):
    count, variables, rows, cols = probes.shape
    edge = jax.ShapeDtypeStruct((count * variables * half // LANES, rows, LANES), BF16)
    tile = lambda at: pl.BlockSpec((count, variables, rows, LANES), lambda _: (0, 0, 0, at))
    kernel = functools.partial(pack_kernel, half, cols)
    return pl.pallas_call(
        kernel,
        grid=(1,),
        out_shape=(edge, edge),
        in_specs=[whole(span), tile(0), tile(cols // LANES - 1)],
        out_specs=(whole(edge), whole(edge)),
        compiler_params=pltpu.CompilerParams(vmem_limit_bytes=16 << 20),
        name="pack",
    )(span, probes, probes)


def prepare_kernel(
    half,
    taps_ref,
    mixing_ref,
    span_ref,
    top_ref,
    bottom_ref,
    near_ref,
    far_ref,
    shore_ref,
    across_ref,
    downward_ref,
    fringe_ref,
):
    probes, variables, _, cols = top_ref.shape
    kernels = downward_ref.shape[0]
    swapped = odd("band")
    low, high = bounds_by_row(span_ref)
    for tile in range(cols // LANES):
        lanes = lanes_of(tile)
        above = land_tile(low[:half], high[:half], tile * LANES)
        below = land_tile(low[-half:], high[-half:], tile * LANES)
        shore_ref[0, :, lanes] = above
        shore_ref[1, :, lanes] = below
        for plane in range(probes * variables):
            at = (plane // variables, plane % variables, slice(None), lanes)
            up, down = top_ref[at] * above, bottom_ref[at] * below
            near_ref[plane, :, lanes] = jnp.where(swapped, up, down)
            far_ref[plane, :, lanes] = jnp.where(swapped, down, up)

    def filtered(kernel, which, distance):
        table = jnp.zeros(distance.shape, F32)
        for tap in range(half + 1):
            table = jnp.where(distance == tap, taps_ref[kernel, which, tap], table)
        return table.astype(BF16)

    def places(shape):
        return lax.broadcasted_iota(jnp.int32, shape, 0), lax.broadcasted_iota(jnp.int32, shape, 1)

    def halves(ref, kernel, first, weight):
        height, width = weight.shape
        parts = ref.shape[2] // width
        for part in range(parts):
            piece = weight.astype(BF16)
            ref[kernel, first : first + height, part * width : (part + 1) * width] = piece
            weight = weight - piece.astype(F32)

    def mixed(kernel, local, v, column, size):
        factor = jnp.zeros(local.shape, F32)
        for w in range(variables):
            factor = jnp.where((column >= w * size) & (column < (w + 1) * size), mixing_ref[kernel, v, w], factor)
        return local * factor

    for kernel in range(kernels):
        row, column = places((across_ref.shape[0], LANES))
        across_ref[:, lanes_of(kernel)] = filtered(kernel, 0, jnp.abs(row - column - half))
        step = downward_ref.shape[1] // variables
        tall = step + 2 * half
        row, column = places((step, variables * tall))
        local = filtered(kernel, 1, jnp.abs((column & (tall - 1)) - half - row)).astype(F32)
        for v in range(variables):
            halves(downward_ref, kernel, v * step, mixed(kernel, local, v, column, tall))
        size = 2 * half
        row, column = places((size, variables * size))
        bits = half.bit_length() - 1
        i, h = row & (half - 1), column & (half - 1)
        upper = (row >> bits) & 1
        gap = jnp.where(upper == 0, i - h, h - i)
        reach = (gap <= 0) & (upper == ((column >> bits) & 1))
        local = filtered(kernel, 1, jnp.where(reach, gap + half, -1)).astype(F32)
        for v in range(variables):
            halves(fringe_ref, kernel, v * size, mixed(kernel, local, v, column, size))


def prepare(probes, taps, mixing, span, half):
    count, variables, rows, cols = probes.shape
    kernels = taps.shape[0]
    size = 2 * half * variables
    strip = jax.ShapeDtypeStruct((count * variables + 1, half, cols), BF16)
    outs = (
        strip,
        strip,
        jax.ShapeDtypeStruct((2, half, cols), BF16),
        jax.ShapeDtypeStruct((2 * LANES, kernels * LANES), BF16),
        jax.ShapeDtypeStruct((kernels, 2 * LANES - 2 * half * variables, PARTS * 2 * LANES), BF16),
        jax.ShapeDtypeStruct((kernels, size, 2 * size), BF16),
    )
    edge = lambda at: pl.BlockSpec((count, variables, half, cols), lambda _: (0, 0, at, 0))
    return pl.pallas_call(
        functools.partial(prepare_kernel, half),
        grid=(1,),
        out_shape=outs,
        in_specs=[SMEM, SMEM, whole(span), edge(0), edge(rows // half - 1)],
        out_specs=tuple(whole(o) for o in outs),
        cost_estimate=pl.CostEstimate(flops=10**7, bytes_accessed=4 << 20, transcendentals=0),
        compiler_params=pltpu.CompilerParams(vmem_limit_bytes=16 << 20),
        name="prepare",
    )(taps, mixing, span, probes, probes)


def corner_kernel(inner_ref, outer_ref, near_in, far_in, near_ref, far_ref):
    half = near_ref.shape[1]
    groups, rows, _ = inner_ref.shape
    swapped = odd("band")
    for at, ref in ((0, inner_ref), (groups, outer_ref)):
        for group in range(groups):
            up, down = ref[group, :half], ref[group, rows - half :]
            near_ref[0, :, lanes_of(at + group)] = jnp.where(swapped, up, down)
            far_ref[0, :, lanes_of(at + group)] = jnp.where(swapped, down, up)
    rest = slice(2 * groups * LANES, near_ref.shape[2])
    near_ref[0, :, rest] = jnp.zeros_like(near_ref[0, :, rest])
    far_ref[0, :, rest] = jnp.zeros_like(far_ref[0, :, rest])


def corner(inner, outer, near, far):
    last = pl.BlockSpec((1, *near.shape[1:]), lambda _: (near.shape[0] - 1, 0, 0))
    keep = pl.BlockSpec(memory_space=pl.ANY)
    return pl.pallas_call(
        corner_kernel,
        grid=(1,),
        out_shape=(jax.ShapeDtypeStruct(near.shape, BF16),) * 2,
        in_specs=[whole(inner), whole(outer), keep, keep],
        out_specs=(last, last),
        input_output_aliases={2: 0, 3: 1},
        compiler_params=pltpu.CompilerParams(vmem_limit_bytes=16 << 20),
        name="corner",
    )(inner, outer, near, far)


def side(block, probe, half, variables):
    per_group = LANES // half // variables
    return pltpu.roll(block.astype(F32), (per_group - probe % per_group) * (half * variables) % LANES, 1)


class Moved:
    def __init__(self, half, height, west, east, tile_of):
        self.half, self.west, self.east, self.tile_of = half, west, east, tile_of
        self.lane = lax.broadcasted_iota(jnp.int32, (height, LANES), 1)
        self.turned = {}

    def turn(self, v, tile):
        if (v, tile) not in self.turned:
            self.turned[v, tile] = pltpu.roll(self.tile_of(v, tile).astype(F32), self.half, 1)
        return self.turned[v, tile]

    def __call__(self, v, tile, tiles):
        half, back = self.half, LANES - self.half * v
        before = self.turn(v, tile - 1) if tile > 0 else pltpu.roll(self.west, back % LANES, 1)
        if tile < tiles:
            after = self.turn(v, tile)
        else:
            after = jnp.where(self.lane < 2 * half, pltpu.roll(self.east, (back + half) % LANES, 1), 0.0)
        return jnp.where(self.lane < half, before, after).astype(BF16)


def fold(part):
    height, width = part.shape
    folded = jnp.sum(part.reshape(height // 8, 8, width), axis=0)
    return sum(folded[:, lanes_of(t)] for t in range(width // LANES))


def own_kernel(
    half,
    nugget_ref,
    span_ref,
    across_ref,
    downward_ref,
    x_ref,
    inner_ref,
    outer_ref,
    out_ref,
    edge_ref,
    sums_ref,
    land_ref,
    ext_ref,
    interior_ref,
):
    probe = pl.program_id(0)
    variables, rows, cols = x_ref.shape[1:]
    kernels = downward_ref.shape[0]
    tiles = cols // LANES

    @pl.when(probe == 0)
    def _():
        low, high = bounds_by_row(span_ref)
        for tile in range(tiles):
            land_ref[:, lanes_of(tile)] = land_tile(low, high, tile * LANES)
        for first in (0, half + rows):
            blank = (slice(None), slice(None), slice(first, first + half), slice(None))
            interior_ref[blank] = jnp.zeros_like(interior_ref[blank])

    group = probe // (LANES // half // variables)
    swapped = odd("region")
    inner, outer = inner_ref[group], outer_ref[group]

    west = side(jnp.where(swapped, inner, outer), probe, half, variables)
    east = side(jnp.where(swapped, outer, inner), probe, half, variables)
    moved = Moved(half, rows, west, east, lambda v, t: x_ref[0, v, :, lanes_of(t)] * land_ref[:, lanes_of(t)])
    sums = [jnp.zeros((8, LANES), F32) for _ in range(kernels + 1)]
    wide = 2 * LANES
    step = downward_ref.shape[1] // variables
    parts = downward_ref.shape[2] // wide

    def filter_columns(chunk):
        first, past = 2 * chunk, 2 * chunk + 2
        for v in range(variables):
            for tile in range(first + (chunk > 0), past + 1):
                ext_ref[v, :, lanes_of(tile)] = moved(v, tile, tiles)
        for tile in range(first, past):
            window = ext_ref[:, :, tile * LANES : (tile + 2) * LANES].reshape(variables * rows, wide)
            both = jnp.dot(window, across_ref[...], preferred_element_type=F32).astype(BF16)
            for kernel in range(kernels):
                interior_ref[kernel, :, half : half + rows, lanes_of(tile)] = both[:, lanes_of(kernel)].reshape(
                    variables, rows, LANES
                )

    def filter_rows(chunk):
        span = slice(chunk * wide, (chunk + 1) * wide)
        for first in range(0, rows, step):
            here = slice(first, first + step)
            terms = []
            for kernel in range(kernels):
                window = interior_ref[kernel, :, first : first + step + 2 * half, span].reshape(wide, wide)
                window = jnp.concatenate([window] * parts, axis=0)
                terms.append(jnp.dot(downward_ref[kernel], window, preferred_element_type=F32))
            land = land_ref[here, span]
            for v in range(variables):
                local = (x_ref[0, v, here, span] * land).astype(F32)
                total = nugget_ref[v] * local
                sums[kernels] = sums[kernels] + fold(total * local)
                for kernel in range(kernels):
                    term = terms[kernel][v * step : (v + 1) * step]
                    sums[kernel] = sums[kernel] + fold(term * local)
                    total = total + term
                out_ref[0, v, here, span] = total.astype(BF16) * land
                if first == 0:
                    edge_ref[0, v, 0, :, span] = total[:half]
                if first + step == rows:
                    edge_ref[0, v, 1, :, span] = total[step - half :]

    filter_columns(0)
    for chunk in range(cols // wide):
        if chunk + 1 < cols // wide:
            filter_columns(chunk + 1)
        filter_rows(chunk)
    for k in range(kernels + 1):
        sums_ref[0, k] = sums[k]


def own(nugget, span, across, downward, probes, inner, outer, half):
    count, variables, rows, cols = probes.shape
    kernels = downward.shape[0]
    block = lambda *shape: pl.BlockSpec((1, *shape), lambda p: (p,) + (0,) * len(shape))
    outs = (
        jax.ShapeDtypeStruct(probes.shape, BF16),
        jax.ShapeDtypeStruct((count, variables, 2, half, cols), F32),
        jax.ShapeDtypeStruct((count, kernels + 1, 8, LANES), F32),
    )
    return pl.pallas_call(
        functools.partial(own_kernel, half),
        grid=(count,),
        out_shape=outs,
        in_specs=[
            SMEM,
            whole(span),
            whole(across),
            whole(downward),
            block(*probes.shape[1:]),
            whole(inner),
            whole(outer),
        ],
        out_specs=tuple(block(*o.shape[1:]) for o in outs),
        scratch_shapes=[
            pltpu.VMEM((rows, cols), BF16),
            pltpu.VMEM((variables, rows, cols + LANES), BF16),
            pltpu.VMEM((kernels, variables, rows + 2 * half, cols), BF16),
        ],
        cost_estimate=pl.CostEstimate(flops=10**10, bytes_accessed=16 << 20, transcendentals=0),
        compiler_params=pltpu.CompilerParams(vmem_limit_bytes=32 << 20),
        name="own",
    )(nugget, span, across, downward, probes, inner, outer)


def border_kernel(
    half,
    across_ref,
    fringe_ref,
    shore_ref,
    near_ref,
    far_ref,
    near_own_ref,
    far_own_ref,
    edge_ref,
    sums_ref,
    base_ref,
    out_ref,
    quad_ref,
    ext_ref,
    ready_ref,
    total_ref,
    sem,
):
    count, variables, _, _, cols = edge_ref.shape
    rows = out_ref.shape[2]
    shares = sums_ref.shape[1]
    kernels = shares - 1
    tiles = cols // LANES
    per_group = LANES // half // variables
    groups = count // per_group
    swapped, flipped = odd("band"), odd("region")
    size = 2 * half * variables
    wide = 2 * LANES
    last = count * variables

    for at in range(2):
        from_near = swapped if at == 0 else jnp.logical_not(swapped)

        def halo(plane, lanes, from_near=from_near):
            return jnp.where(from_near, near_ref[plane, :, lanes], far_ref[plane, :, lanes])

        for p in range(count):
            inner, outer = (halo(last, lanes_of(kind + p // per_group)) for kind in (0, groups))
            west = side(jnp.where(flipped, inner, outer), p, half, variables)
            east = side(jnp.where(flipped, outer, inner), p, half, variables)
            moved = Moved(half, half, west, east, lambda v, t, p=p: halo(p * variables + v, lanes_of(t)))
            for v in range(variables):
                first = (2 * v + at) * half
                for tile in range(tiles + 1):
                    ext_ref[p, first : first + half, lanes_of(tile)] = moved(v, tile, tiles)

    def filter_columns(tile):
        window = ext_ref[:, :, tile * LANES : (tile + 2) * LANES].reshape(count * size, wide)
        both = jnp.dot(window, across_ref[...], preferred_element_type=F32).astype(BF16)
        for kernel in range(kernels):
            piece = both[:, lanes_of(kernel)].reshape(count, size, LANES)
            ready_ref[kernel, :, :size, lanes_of(tile)] = piece
            ready_ref[kernel, :, size:, lanes_of(tile)] = piece

    sums = {(p, k): sums_ref[p, k] for p in range(count) for k in range(shares)}

    def filter_rows(chunk):
        span = slice(chunk * wide, (chunk + 1) * wide)
        shore = shore_ref[:, :, span]
        for p in range(count):
            planes = slice(p * variables, (p + 1) * variables)
            near, far = near_own_ref[planes, :, span], far_own_ref[planes, :, span]
            up, down = jnp.where(swapped, near, far), jnp.where(swapped, far, near)
            total = edge_ref[p, :, :, :, span]
            local = jnp.concatenate([up[:, None], down[:, None]], axis=1).astype(F32)
            for kernel in range(kernels):
                term = jnp.dot(fringe_ref[kernel], ready_ref[kernel, p, :, span], preferred_element_type=F32)
                sums[p, kernel] = sums[p, kernel] + fold(term * local.reshape(size, wide))
                total = total + term.reshape(total.shape)
            total_ref[p, :, :, :, span] = total.astype(BF16) * shore[None]

    chunks = cols // wide
    for tile in (0, 1):
        filter_columns(tile)
    for chunk in range(chunks):
        for tile in (2 * chunk + 2, 2 * chunk + 3):
            if tile < tiles:
                filter_columns(tile)
        filter_rows(chunk)

    copies = [
        pltpu.make_async_copy(total_ref.at[:, :, at], out_ref.at[:, :, pl.ds(first, half), :], sem.at[at])
        for at, first in ((0, 0), (1, rows - half))
    ]
    for copy in copies:
        copy.start()

    lane = lax.broadcasted_iota(jnp.int32, quad_ref.shape, 1)
    line = jnp.zeros(quad_ref.shape, F32)
    for (p, k), part in sums.items():
        line = jnp.where(lane == p * shares + k, jnp.sum(part), line)
    quad_ref[...] = line
    for copy in copies:
        copy.wait()


def border(across, fringe, shore, near, far, near_own, far_own, edge, sums, base, half, devices):
    count, variables, rows, cols = base.shape
    kernels = fringe.shape[0]
    size = 2 * half * variables
    keep = pl.BlockSpec(memory_space=pl.ANY)
    quads = jax.ShapeDtypeStruct((devices, LANES), F32)
    operands = (across, fringe, shore, near, far, near_own, far_own, edge, sums)
    return pl.pallas_call(
        functools.partial(border_kernel, half),
        grid=(1,),
        out_shape=(jax.ShapeDtypeStruct(base.shape, BF16), quads),
        in_specs=[whole(o) for o in operands] + [keep],
        out_specs=(keep, whole(quads)),
        scratch_shapes=[
            pltpu.VMEM((count, size, cols + LANES), BF16),
            pltpu.VMEM((kernels, count, 2 * size, cols), BF16),
            pltpu.VMEM((count, variables, 2, half, cols), BF16),
            pltpu.SemaphoreType.DMA((2,)),
        ],
        input_output_aliases={len(operands): 0},
        compiler_params=pltpu.CompilerParams(vmem_limit_bytes=32 << 20),
        name="border",
    )(*operands, base)


def per_device(probes, filter_taps, mixing, nugget, land_span):
    count, variables, rows, cols = probes.shape
    kernels = filter_taps.shape[0]
    half = filter_taps.shape[2] - 1
    regions, bands = lax.axis_size("region"), lax.axis_size("band")
    inner_pairs = [(i, i ^ 1) for i in range(regions)]
    outer_pairs = [(i, (i + 1 if i % 2 else i - 1) % regions) for i in range(regions)]
    near_pairs = [(i, i ^ 1) for i in range(bands)]
    far_pairs = [(i, i + 1 if i % 2 else i - 1) for i in range(1, bands - 1)]

    probes = pltpu.with_memory_space_constraint(probes, pltpu.HBM)
    span = pltpu.with_memory_space_constraint(land_span.reshape(2, 1, rows), pltpu.HBM)
    inner, outer = pack(probes, span, half)
    inner = lax.ppermute(inner, "region", inner_pairs)
    outer = lax.ppermute(outer, "region", outer_pairs)
    near, far, shore, across, downward, fringe = prepare(probes, filter_taps, mixing, span, half)
    near, far = corner(inner, outer, near, far)
    near_halo = lax.ppermute(near, "band", near_pairs)
    far_halo = lax.ppermute(far, "band", far_pairs)
    base, edge, sums = own(nugget, span, across, downward, probes, inner, outer, half)
    output, quads = border(
        across, fringe, shore, near_halo, far_halo, near, far, edge, sums, base, half, regions * bands
    )
    shares = lax.all_to_all(quads, ("region", "band"), 0, 0, tiled=True)
    quadratic = jnp.sum(shares, axis=0)[: count * (kernels + 1)].reshape(count, kernels + 1)
    return output, quadratic / (bands * rows * cols)


def solution(mesh):
    in_specs = (P(None, None, "band", "region"), P(), P(), P(), P(None, "band", "region"))
    out_specs = (P(None, None, "band", "region"), P())
    return jax.shard_map(
        per_device, mesh=mesh, in_specs=in_specs, out_specs=out_specs, check_vma=False
    )
```

time: 47.9 us -> 41.9 us (0.87)
  Pallas kernels: 23.6 us -> 17.8 us
  local copies, waits for them, and re-layouts: 1.35 us -> 0.68 us
    pallas_call x1, Pallas kernels: 15.3 us -> 11.1 us  [own(): pl.pallas_call(functools.partial(own_kernel, half), grid=(count,), out_sh...]
    pallas_call x1, Pallas kernels: 4.19 us -> 3.1 us  [border(): pl.pallas_call(functools.partial(border_kernel, half), grid=(1,), out_sha...]
    unnamed x10 -> x6, local copies, waits for them, and re-layouts: 0.69 us -> 0.01 us
  transfers between devices with their start and end apart: 4 -> 4, of which waited for: 1 -> 1; matrix products, arithmetic and copies ran while one was open for 0% -> 0% of each run, Pallas kernels for 37% -> 31%
where the time goes in v3:
time: 41.9 us; the launch traced here: 41.7 us
  Pallas kernels  17.8 us (42%)
  blocking collectives  13.7 us (33%)
  starting transfers between devices  7.37 us (18%)
  waiting for transfers between devices  1.33 us (3%)
  between operations  0.71 us (2%)
  local copies, waits for them, and re-layouts  0.68 us (2%)
    all_to_all x1, blocking collectives, per_device(): shares = lax.all_to_all(quads, ('region', 'band'), 0, 0, tiled=True)  13.7 us
    pallas_call x1, Pallas kernels, own(): pl.pallas_call(functools.partial(own_kernel, half), grid=(count,), out_sh...  11.1 us
    ppermute x1, starting transfers between devices, per_device(): outer = lax.ppermute(outer, 'region', outer_pairs)  3.57 us
    pallas_call x1, Pallas kernels, border(): pl.pallas_call(functools.partial(border_kernel, half), grid=(1,), out_sha...  3.1 us
    ppermute x1, starting transfers between devices, per_device(): inner = lax.ppermute(inner, 'region', inner_pairs)  3.03 us
    pallas_call x1, Pallas kernels, prepare(): pl.pallas_call(functools.partial(prepare_kernel, half), grid=(1,), out_sh...  2.04 us
    pallas_call x1, Pallas kernels, pack(): pl.pallas_call(kernel, grid=(1,), out_shape=(edge, edge), in_specs=[whole...  1.63 us
    ppermute x1, waiting for transfers between devices, per_device(): outer = lax.ppermute(outer, 'region', outer_pairs)  1.32 us
  transfers between devices with their start and end apart: 4, of which 1 were waited for; matrix products, arithmetic and copies ran while one was open for 0% of the time, Pallas kernels for 31%

profile of v3, /device:TPU:0, one launch (start us, length us, event | category | flops | bytes accessed | tf_op | source)
XLA Modules:
  0.0 41.7 jit_solution(5357248974194567624)
XLA Ops:
  0.6 0.0 copy-start
  0.6 0.0 copy-start.1
  0.6 1.6 %pack.1 = (bf16[2,128,128]{2,1,0:T(8,128)(2,1)S(1)}, bf16[2,128,128]{2,1,0:T(8,128)(2,1)S(1)}) custom-call(s32[2,1,128]{2,1,0:T(1,128)} %bitcast.5, bf16[4,4,128,1024]{3,2,1,0:T(8,128)(2,1)} %x_ref.1, bf16[4,4,128,1024]{3,2,1,0:T(8,128)(2,1)} %x_ref.1), custom_call_target="tpu_custom_call" | custom-call | tf_op jit(solution)/shard_map/pack/pallas_call | solution.py:61
  2.3 3.0 %collective-permute-start = (bf16[2,128,128]{2,1,0:T(8,128)(2,1)S(1)}, bf16[2,128,128]{2,1,0:T(8,128)(2,1)S(1)}, u32[]{:S(2)}, u32[]{:S(2)}) collective-permute-start(bf16[2,128,128]{2,1,0:T(8,128)(2,1)S(1)} %get-tuple-element.20), channel_id=1, source_target_pairs={{0,4},{4,0},{8,12},{12,8},{16,20},{20,16},{24,28},{28,24},{1,5},{5... | collective-permute-start | bytes 196616 | tf_op jit(solution)/shard_map/ppermute | solution.py:490
  5.3 0.0 copy-start.2
  5.3 3.6 %collective-permute-start.1 = (bf16[2,128,128]{2,1,0:T(8,128)(2,1)S(1)}, bf16[2,128,128]{2,1,0:T(8,128)(2,1)S(1)}, u32[]{:S(2)}, u32[]{:S(2)}) collective-permute-start(bf16[2,128,128]{2,1,0:T(8,128)(2,1)S(1)} %get-tuple-element.21), channel_id=1, source_target_pairs={{0,28},{4,8},{8,4},{12,16},{16,12},{20,24},{24,20},{28,0},{1,29},{... | collective-permute-start | bytes 196616 | tf_op jit(solution)/shard_map/ppermute | solution.py:491
  8.9 0.0 copy-done
  8.9 0.0 copy-done.1
  8.9 2.0 %prepare.1 = (bf16[17,16,1024]{2,1,0:T(8,128)(2,1)S(1)}, bf16[17,16,1024]{2,1,0:T(8,128)(2,1)S(1)}, bf16[2,16,1024]{2,1,0:T(8,128)(2,1)S(1)}, bf16[256,256]{1,0:...) custom-call(f32[2,2,17]{2,1,0:T(2,128)S(1)} %copy-done.1, f32[2,4,4]{2,1,0:T(4,128)S(1)} %copy-done, ...), custom_call_target="tpu_custom_call" | custom-call | flops 10000000 | bytes 4194304 | tf_op jit(solution)/shard_map/prepare/pallas_call | solution.py:160
  11.0 0.0 collective-permute-done.inner_ref
  11.0 1.3 %collective-permute-done.1.outer_ref = bf16[2,128,128]{2,1,0:T(8,128)(2,1)S(1)} collective-permute-done((bf16[2,128,128]{2,1,0:T(8,128)(2,1)S(1)}, bf16[2,128,128]{2,1,0:T(8,128)(2,1)S(1)}, u32[]{:S(2)}, u32[]{:S(2)}) %collective-permute-start.1) | collective-permute-done | bytes 65568 | tf_op jit(solution)/shard_map/ppermute | solution.py:491
  12.3 0.1 collective-permute-start.2
  12.4 0.7 %collective-permute-start.3 = (bf16[17,16,1024]{2,1,0:T(8,128)(2,1)S(1)}, bf16[17,16,1024]{2,1,0:T(8,128)(2,1)S(1)}, u32[]{:S(2)}, u32[]{:S(2)}) collective-permute-start(bf16[17,16,1024]{2,1,0:T(8,128)(2,1)S(1)} %get-tuple-element.25.far_own_ref), channel_id=1, source_target_pairs={{1,2},{2,1},{5,6},{6,5},{9,10},{10,9},{13,14},{14,13},{17,18},{18,... | collective-permute-start | bytes 1671176 | tf_op jit(solution)/shard_map/ppermute | solution.py:495
  13.1 0.0 copy-done.2
  13.1 11.1 %own.1 = (bf16[4,4,128,1024]{3,2,1,0:T(8,128)(2,1)}, f32[4,4,2,16,1024]{4,3,2,1,0:T(8,128)S(1)}, f32[4,3,8,128]{3,2,1,0:T(8,128)S(1)}) custom-call(f32[4]{0:T(128)S(1)} %copy-done.2, s32[2,1,128]{2,1,0:T(1,128)} %bitcast.7, bf16[256,256]{1,0:T(8,128)(2,1)S(1)} %get-tuple-element.17.across_ref, bf16[2,128,256]{2,1,0:T(8,128)(2,1)S(1)} %get-tuple-element.26.downward_ref, ...), custom_call_target="tpu_custom_call" | custom-call | flops 10000000000 | bytes 16777216 | tf_op jit(solution)/shard_map/own/pallas_call | solution.py:330
  24.1 0.0 collective-permute-done.2.near_ref
  24.2 0.0 collective-permute-done.3.far_ref
  24.2 3.1 %border.1 = (bf16[4,4,128,1024]{3,2,1,0:T(8,128)(2,1)}, f32[32,128]{1,0:T(8,128)S(1)}) custom-call(bf16[256,256]{1,0:T(8,128)(2,1)S(1)} %get-tuple-element.17.across_ref, bf16[2,128,256]{2,1,0:T(8,128)(2,1)S(1)} %get-tuple-element.18.fringe_ref, bf16[2,16,1024]{2,1,0:T(8,128)(2,1)S(1)} %get-tuple-element.19.shore_ref, ...), custom_call_target="tpu_custom_call", output_to_operand_aliasing={{0}: (9, {})} | custom-call | tf_op jit(solution)/shard_map/border/pallas_call | solution.py:459
  27.3 13.7 %all_to_all.9 = f32[32,1,128]{2,1,0:T(1,128)S(1)} all-to-all(f32[32,1,128]{2,1,0:T(1,128)S(1)} %bitcast.4), channel_id=1, replica_groups=mesh['region'=8,'band'=4] {'region','band'}, dimensions={0} | all-to-all | bytes 32768 | tf_op jit(solution)/shard_map/all_to_all | solution.py:500
  40.9 0.1 reduce_sum.9
  41.0 0.7 %div.6 = f32[4,3]{1,0:T(4,128)} reshape(f32[12]{0:T(128)S(1)} %slice_multiply_fusion) | data formatting | bytes 96 | tf_op jit(solution)/shard_map/div | solution.py:502
  (2 shorter events, 0.0 us)
Async XLA Ops:
  0.6 8.3 %copy-start = (f32[2,4,4]{2,1,0:T(4,128)S(1)}, f32[2,4,4]{2,1,0:T(4,128)}, u32[]{:S(2)}) copy-start(f32[2,4,4]{2,1,0:T(4,128)} %mixing_ref.1) | copy-start | bytes 388
  0.6 8.3 %copy-start.1 = (f32[2,2,17]{2,1,0:T(2,128)S(1)}, f32[2,2,17]{2,1,0:T(2,128)}, u32[]{:S(2)}) copy-start(f32[2,2,17]{2,1,0:T(2,128)} %taps_ref.1) | copy-start | bytes 820
  2.3 8.7 %collective-permute-start = (bf16[2,128,128]{2,1,0:T(8,128)(2,1)S(1)}, bf16[2,128,128]{2,1,0:T(8,128)(2,1)S(1)}, u32[]{:S(2)}, u32[]{:S(2)}) collective-permute-start(bf16[2,128,128]{2,1,0:T(8,128)(2,1)S(1)} %get-tuple-element.20), channel_id=1, source_target_pairs={{0,4},{4,0},{8,12},{12,8},{16,20},{20,16},{24,28},{28,24},{1,5},{5... | collective-permute-start | bytes 196616 | tf_op jit(solution)/shard_map/ppermute | solution.py:490
  5.3 7.8 %copy-start.2 = (f32[4]{0:T(128)S(1)}, f32[4]{0:T(128)}, u32[]{:S(2)}) copy-start(f32[4]{0:T(128)} %nugget_ref.1) | copy-start | bytes 52
  5.3 7.0 %collective-permute-start.1 = (bf16[2,128,128]{2,1,0:T(8,128)(2,1)S(1)}, bf16[2,128,128]{2,1,0:T(8,128)(2,1)S(1)}, u32[]{:S(2)}, u32[]{:S(2)}) collective-permute-start(bf16[2,128,128]{2,1,0:T(8,128)(2,1)S(1)} %get-tuple-element.21), channel_id=1, source_target_pairs={{0,28},{4,8},{8,4},{12,16},{16,12},{20,24},{24,20},{28,0},{1,29},{... | collective-permute-start | bytes 196616 | tf_op jit(solution)/shard_map/ppermute | solution.py:491
  12.3 11.8 %collective-permute-start.2 = (bf16[17,16,1024]{2,1,0:T(8,128)(2,1)S(1)}, bf16[17,16,1024]{2,1,0:T(8,128)(2,1)S(1)}, u32[]{:S(2)}, u32[]{:S(2)}) collective-permute-start(bf16[17,16,1024]{2,1,0:T(8,128)(2,1)S(1)} %get-tuple-element.24.near_own_ref), channel_id=1, source_target_pairs={{0,1},{1,0},{2,3},{3,2},{4,5},{5,4},{6,7},{7,6},{8,9},{9,8},{10,11... | collective-permute-start | bytes 1671176 | tf_op jit(solution)/shard_map/ppermute | solution.py:494
  12.4 11.8 %collective-permute-start.3 = (bf16[17,16,1024]{2,1,0:T(8,128)(2,1)S(1)}, bf16[17,16,1024]{2,1,0:T(8,128)(2,1)S(1)}, u32[]{:S(2)}, u32[]{:S(2)}) collective-permute-start(bf16[17,16,1024]{2,1,0:T(8,128)(2,1)S(1)} %get-tuple-element.25.far_own_ref), channel_id=1, source_target_pairs={{1,2},{2,1},{5,6},{6,5},{9,10},{10,9},{13,14},{14,13},{17,18},{18,... | collective-permute-start | bytes 1671176 | tf_op jit(solution)/shard_map/ppermute | solution.py:495

commit v4 on v3

v4 whole, which is shorter than its diff:
```python
import functools

import jax
import jax.numpy as jnp
from jax import lax
from jax.experimental import pallas as pl
from jax.experimental.pallas import tpu as pltpu
from jax.sharding import PartitionSpec as P

LANES = 128
BF16 = jnp.bfloat16
F32 = jnp.float32
PARTS = 1
SMEM = pl.BlockSpec(memory_space=pltpu.SMEM)


def lanes_of(tile):
    return slice(tile * LANES, (tile + 1) * LANES)


def whole(a):
    return pl.BlockSpec(a.shape, lambda *_: (0,) * len(a.shape))


def odd(axis):
    return lax.axis_index(axis) % 2 != 0


def bounds_by_row(span_ref):
    return [jnp.broadcast_to(span_ref[entry].astype(F32), (LANES, LANES)).T for entry in range(2)]


def land_tile(low, high, first_col):
    column = (lax.broadcasted_iota(jnp.int32, low.shape, 1) + first_col).astype(F32)
    return ((column >= low) & (column < high)).astype(F32).astype(BF16)


def pack_kernel(half, cols, outer, span_ref, x_ref, edge_ref, tile_ref, sem):
    _, variables, _, _ = x_ref.shape
    per_group = LANES // half
    east = odd("region") == outer
    first = pl.multiple_of(jnp.where(east, cols - LANES, 0), LANES)
    copy = pltpu.make_async_copy(x_ref.at[:, :, :, pl.ds(first, LANES)], tile_ref, sem)
    copy.start()
    low, high = bounds_by_row(span_ref)
    land = land_tile(low, high, first)
    copy.wait()
    for group in range(edge_ref.shape[0]):
        pieces = []
        for plane in range(group * per_group, (group + 1) * per_group):
            tile = tile_ref[plane // variables, plane % variables] * land
            pieces.append(jnp.where(east, tile[:, LANES - half :], tile[:, :half]))
        edge_ref[group] = jnp.concatenate(pieces, axis=1)


def pack(probes, span, half, outer):
    count, variables, rows, cols = probes.shape
    edge = jax.ShapeDtypeStruct((count * variables * half // LANES, rows, LANES), BF16)
    return pl.pallas_call(
        functools.partial(pack_kernel, half, cols, outer),
        grid=(1,),
        out_shape=edge,
        in_specs=[whole(span), pl.BlockSpec(memory_space=pl.ANY)],
        out_specs=whole(edge),
        scratch_shapes=[pltpu.VMEM((count, variables, rows, LANES), BF16), pltpu.SemaphoreType.DMA],
        cost_estimate=pl.CostEstimate(flops=10**6, bytes_accessed=1 << 20, transcendentals=0),
        compiler_params=pltpu.CompilerParams(vmem_limit_bytes=16 << 20),
        name="pack",
    )(span, probes)


def prepare_kernel(
    half,
    taps_ref,
    mixing_ref,
    span_ref,
    x_ref,
    masked_ref,
    near_ref,
    far_ref,
    land_ref,
    across_ref,
    downward_ref,
    fringe_ref,
):
    probe = pl.program_id(0)
    variables, rows, cols = x_ref.shape[1:]
    tiles = cols // LANES
    swapped = odd("band")

    @pl.when(probe == 0)
    def _():
        low, high = bounds_by_row(span_ref)
        for tile in range(tiles):
            land_ref[tile] = land_tile(low, high, tile * LANES)

    for tile in range(tiles):
        land = land_ref[tile]
        for v in range(variables):
            plane = probe * variables + v
            value = x_ref[0, v, :, lanes_of(tile)] * land
            masked_ref[plane, tile] = value
            up, down = value[:half], value[rows - half :]
            near_ref[plane, tile] = jnp.where(swapped, up, down)
            far_ref[plane, tile] = jnp.where(swapped, down, up)

    @pl.when(probe == pl.num_programs(0) - 1)
    def _():
        make_tables(half, variables, taps_ref, mixing_ref, across_ref, downward_ref, fringe_ref)


def make_tables(half, variables, taps_ref, mixing_ref, across_ref, downward_ref, fringe_ref):
    kernels = downward_ref.shape[0]
    swapped = odd("band")

    def filtered(kernel, which, distance):
        table = jnp.zeros(distance.shape, F32)
        for tap in range(half + 1):
            table = jnp.where(distance == tap, taps_ref[kernel, which, tap], table)
        return table.astype(BF16)

    def places(shape):
        return lax.broadcasted_iota(jnp.int32, shape, 0), lax.broadcasted_iota(jnp.int32, shape, 1)

    def halves(ref, kernel, first, weight):
        height, width = weight.shape
        parts = ref.shape[2] // width
        for part in range(parts):
            piece = weight.astype(BF16)
            ref[kernel, first : first + height, part * width : (part + 1) * width] = piece
            weight = weight - piece.astype(F32)

    def mixed(kernel, local, v, column, size):
        factor = jnp.zeros(local.shape, F32)
        for w in range(variables):
            factor = jnp.where((column >= w * size) & (column < (w + 1) * size), mixing_ref[kernel, v, w], factor)
        return local * factor

    for kernel in range(kernels):
        row, column = places((LANES, LANES))
        across_ref[:LANES, lanes_of(kernel)] = filtered(kernel, 0, jnp.abs(row - column))
        gap = jnp.where(row < LANES // 2, LANES + row - column, LANES - row + column)
        across_ref[LANES:, lanes_of(kernel)] = filtered(kernel, 0, gap)
        step = downward_ref.shape[1] // variables
        tall = step + 2 * half
        row, column = places((step, variables * tall))
        local = filtered(kernel, 1, jnp.abs((column & (tall - 1)) - half - row)).astype(F32)
        for v in range(variables):
            halves(downward_ref, kernel, v * step, mixed(kernel, local, v, column, tall))
        size = 2 * half
        row, column = places((size, variables * size))
        bits = half.bit_length() - 1
        i, h = row & (half - 1), column & (half - 1)
        which = (row >> bits) & 1
        gap = jnp.where((which == 0) == swapped, i - h, h - i)
        reach = (gap <= 0) & (which == ((column >> bits) & 1))
        local = filtered(kernel, 1, jnp.where(reach, gap + half, -1)).astype(F32)
        for v in range(variables):
            halves(fringe_ref, kernel, v * size, mixed(kernel, local, v, column, size))


def prepare(probes, taps, mixing, span, half):
    count, variables, rows, cols = probes.shape
    kernels = taps.shape[0]
    planes, tiles = count * variables, cols // LANES
    size = 2 * half * variables
    strip = jax.ShapeDtypeStruct((planes + 1, tiles, half, LANES), BF16)
    outs = (
        jax.ShapeDtypeStruct((planes, tiles, rows, LANES), BF16),
        strip,
        strip,
        jax.ShapeDtypeStruct((tiles, rows, LANES), BF16),
        jax.ShapeDtypeStruct((2 * LANES, kernels * LANES), BF16),
        jax.ShapeDtypeStruct((kernels, 2 * LANES - 2 * half * variables, PARTS * 2 * LANES), BF16),
        jax.ShapeDtypeStruct((kernels, size, PARTS * size), BF16),
    )
    return pl.pallas_call(
        functools.partial(prepare_kernel, half),
        grid=(count,),
        out_shape=outs,
        in_specs=[SMEM, SMEM, whole(span), pl.BlockSpec((1, *probes.shape[1:]), lambda p: (p, 0, 0, 0))],
        out_specs=tuple(whole(o) for o in outs),
        cost_estimate=pl.CostEstimate(flops=10**7, bytes_accessed=4 << 20, transcendentals=0),
        compiler_params=pltpu.CompilerParams(vmem_limit_bytes=16 << 20),
        name="prepare",
    )(taps, mixing, span, probes)


def corner_kernel(inner_ref, outer_ref, near_in, far_in, near_ref, far_ref):
    tiles, half = near_ref.shape[1:3]
    groups, rows, _ = inner_ref.shape
    swapped = odd("band")
    for at, ref in ((0, inner_ref), (groups, outer_ref)):
        for group in range(groups):
            up, down = ref[group, :half], ref[group, rows - half :]
            near_ref[0, at + group] = jnp.where(swapped, up, down)
            far_ref[0, at + group] = jnp.where(swapped, down, up)
    for tile in range(2 * groups, tiles):
        near_ref[0, tile] = jnp.zeros_like(near_ref[0, tile])
        far_ref[0, tile] = jnp.zeros_like(far_ref[0, tile])


def corner(inner, outer, near, far):
    last = pl.BlockSpec((1, *near.shape[1:]), lambda _: (near.shape[0] - 1, 0, 0, 0))
    keep = pl.BlockSpec(memory_space=pl.ANY)
    return pl.pallas_call(
        corner_kernel,
        grid=(1,),
        out_shape=(jax.ShapeDtypeStruct(near.shape, BF16),) * 2,
        in_specs=[whole(inner), whole(outer), keep, keep],
        out_specs=(last, last),
        input_output_aliases={2: 0, 3: 1},
        compiler_params=pltpu.CompilerParams(vmem_limit_bytes=16 << 20),
        name="corner",
    )(inner, outer, near, far)


def around(tile_of, v, tile, tiles, west, east, probe, half, variables):
    slot = (probe % (LANES // half // variables)) * variables + v

    def line_up(block, lane):
        return pltpu.roll(block.astype(F32), (lane + LANES - half * slot) % LANES, 1).astype(BF16)

    before = tile_of(v, tile - 1) if tile > 0 else line_up(west, LANES - half)
    after = tile_of(v, tile + 1) if tile + 1 < tiles else line_up(east, 0)
    lane = lax.broadcasted_iota(jnp.int32, before.shape, 1)
    return jnp.where(lane < LANES // 2, after, before)


def fold(part):
    height, width = part.shape
    folded = jnp.sum(part.reshape(height // 8, 8, width), axis=0)
    return sum(folded[:, lanes_of(t)] for t in range(width // LANES))


def own_kernel(
    half,
    nugget_ref,
    across_ref,
    downward_ref,
    masked_ref,
    land_ref,
    inner_ref,
    outer_ref,
    out_ref,
    edge_ref,
    sums_ref,
    interior_ref,
):
    probe = pl.program_id(0)
    variables, rows, cols = out_ref.shape[1:]
    kernels = downward_ref.shape[0]
    tiles = cols // LANES
    upper = jnp.where(odd("band"), 0, 1)

    @pl.when(probe == 0)
    def _():
        for first in (0, half + rows):
            blank = (slice(None),) * 3 + (slice(first, first + half), slice(None))
            interior_ref[blank] = jnp.zeros_like(interior_ref[blank])

    group = probe // (LANES // half // variables)
    swapped = odd("region")
    inner, outer = inner_ref[group], outer_ref[group]

    west, east = jnp.where(swapped, inner, outer), jnp.where(swapped, outer, inner)

    def tile_of(v, tile):
        return masked_ref[probe * variables + v, tile]

    sums = [jnp.zeros((8, LANES), F32) for _ in range(kernels + 1)]
    wide = 2 * LANES
    step = downward_ref.shape[1] // variables
    parts = downward_ref.shape[2] // wide

    def filter_columns(chunk):
        for tile in (2 * chunk, 2 * chunk + 1):
            window = []
            for v in range(variables):
                sides = around(tile_of, v, tile, tiles, west, east, probe, half, variables)
                window.append(jnp.concatenate([tile_of(v, tile), sides], axis=1))
            window = jnp.concatenate(window, axis=0)
            both = jnp.dot(window, across_ref[...], preferred_element_type=F32).astype(BF16)
            for kernel in range(kernels):
                interior_ref[kernel, :, tile, half : half + rows] = both[:, lanes_of(kernel)].reshape(
                    variables, rows, LANES
                )

    def filter_rows(chunk):
        span = slice(chunk * wide, (chunk + 1) * wide)
        for first in range(0, rows, step):
            here = slice(first, first + step)
            terms = []
            for kernel in range(kernels):
                window = jnp.concatenate(
                    [
                        interior_ref[kernel, :, tile, first : first + step + 2 * half].reshape(wide, LANES)
                        for tile in (2 * chunk, 2 * chunk + 1)
                    ],
                    axis=1,
                )
                window = jnp.concatenate([window] * parts, axis=0)
                terms.append(jnp.dot(downward_ref[kernel], window, preferred_element_type=F32))
            land = jnp.concatenate([land_ref[2 * chunk, here], land_ref[2 * chunk + 1, here]], axis=1)
            for v in range(variables):
                plane = probe * variables + v
                local = jnp.concatenate(
                    [masked_ref[plane, 2 * chunk, here], masked_ref[plane, 2 * chunk + 1, here]], axis=1
                ).astype(F32)
                total = nugget_ref[v] * local
                sums[kernels] = sums[kernels] + fold(total * local)
                for kernel in range(kernels):
                    term = terms[kernel][v * step : (v + 1) * step]
                    sums[kernel] = sums[kernel] + fold(term * local)
                    total = total + term
                out_ref[0, v, here, span] = total.astype(BF16) * land
                if first == 0:
                    edge_ref[0, v, upper, :, span] = total[:half]
                if first + step == rows:
                    edge_ref[0, v, 1 - upper, :, span] = total[step - half :]

    filter_columns(0)
    for chunk in range(cols // wide):
        if chunk + 1 < cols // wide:
            filter_columns(chunk + 1)
        filter_rows(chunk)
    for k in range(kernels + 1):
        sums_ref[0, k] = sums[k]


def own(nugget, across, downward, masked, land, inner, outer, half, shape):
    count, variables, rows, cols = shape
    kernels = downward.shape[0]
    block = lambda *shape: pl.BlockSpec((1, *shape), lambda p: (p,) + (0,) * len(shape))
    outs = (
        jax.ShapeDtypeStruct(shape, BF16),
        jax.ShapeDtypeStruct((count, variables, 2, half, cols), F32),
        jax.ShapeDtypeStruct((count, kernels + 1, 8, LANES), F32),
    )
    operands = (across, downward, masked, land, inner, outer)
    return pl.pallas_call(
        functools.partial(own_kernel, half),
        grid=(count,),
        out_shape=outs,
        in_specs=[SMEM] + [whole(o) for o in operands],
        out_specs=tuple(block(*o.shape[1:]) for o in outs),
        scratch_shapes=[pltpu.VMEM((kernels, variables, cols // LANES, rows + 2 * half, LANES), BF16)],
        cost_estimate=pl.CostEstimate(flops=10**10, bytes_accessed=16 << 20, transcendentals=0),
        compiler_params=pltpu.CompilerParams(vmem_limit_bytes=32 << 20),
        name="own",
    )(nugget, *operands)


def border_kernel(
    half,
    across_ref,
    fringe_ref,
    land_ref,
    near_ref,
    far_ref,
    near_own_ref,
    far_own_ref,
    edge_ref,
    sums_ref,
    base_ref,
    out_ref,
    quad_ref,
    ready_ref,
    total_ref,
    sem,
):
    count, variables, _, _, cols = edge_ref.shape
    rows = out_ref.shape[2]
    shares = sums_ref.shape[1]
    kernels = shares - 1
    tiles = cols // LANES
    per_group = LANES // half // variables
    groups = count // per_group
    flipped = odd("region")
    upper = jnp.where(odd("band"), 0, rows - half)
    firsts = [pl.multiple_of(upper, half), pl.multiple_of(rows - half - upper, half)]
    size = 2 * half * variables
    wide = 2 * LANES
    last = count * variables

    halos = (near_ref, far_ref)

    def corners(ref, p):
        inner, outer = (ref[last, kind + p // per_group] for kind in (0, groups))
        return jnp.where(flipped, inner, outer), jnp.where(flipped, outer, inner)

    ends = {(at, p): corners(halos[at], p) for at in range(2) for p in range(count)}

    def filter_columns(tile):
        window = []
        for p in range(count):
            for v in range(variables):
                for at in range(2):
                    tile_of = lambda v, t: halos[at][p * variables + v, t]
                    sides = around(tile_of, v, tile, tiles, *ends[at, p], p, half, variables)
                    window.append(jnp.concatenate([tile_of(v, tile), sides], axis=1))
        window = jnp.concatenate(window, axis=0)
        both = jnp.dot(window, across_ref[...], preferred_element_type=F32).astype(BF16)
        for kernel in range(kernels):
            piece = both[:, lanes_of(kernel)].reshape(count, size, LANES)
            ready_ref[kernel, :, tile] = piece

    sums = {(p, k): sums_ref[p, k] for p in range(count) for k in range(shares)}

    def filter_rows(chunk):
        span = slice(chunk * wide, (chunk + 1) * wide)
        pair = (2 * chunk, 2 * chunk + 1)
        strips = [
            jnp.concatenate([land_ref[tile, pl.ds(first, half)] for tile in pair], axis=1) for first in firsts
        ]
        shore = jnp.stack(strips)
        for p in range(count):
            planes = slice(p * variables, (p + 1) * variables)
            near, far = (
                jnp.concatenate([ref[planes, tile] for tile in pair], axis=2) for ref in (near_own_ref, far_own_ref)
            )
            total = edge_ref[p, :, :, :, span]
            local = jnp.stack([near, far], axis=1).astype(F32)
            for kernel in range(kernels):
                window = jnp.concatenate([ready_ref[kernel, p, tile] for tile in pair], axis=1)
                window = jnp.concatenate([window] * (fringe_ref.shape[2] // size), axis=0)
                term = jnp.dot(fringe_ref[kernel], window, preferred_element_type=F32)
                sums[p, kernel] = sums[p, kernel] + fold(term * local.reshape(size, wide))
                total = total + term.reshape(total.shape)
            total_ref[p, :, :, :, span] = total.astype(BF16) * shore[None]

    chunks = cols // wide
    for tile in (0, 1):
        filter_columns(tile)
    for chunk in range(chunks):
        for tile in (2 * chunk + 2, 2 * chunk + 3):
            if tile < tiles:
                filter_columns(tile)
        filter_rows(chunk)

    copies = [
        pltpu.make_async_copy(total_ref.at[:, :, at], out_ref.at[:, :, pl.ds(first, half), :], sem.at[at])
        for at, first in enumerate(firsts)
    ]
    for copy in copies:
        copy.start()

    lane = lax.broadcasted_iota(jnp.int32, quad_ref.shape, 1)
    line = jnp.zeros(quad_ref.shape, F32)
    for (p, k), part in sums.items():
        line = jnp.where(lane == p * shares + k, jnp.sum(part), line)
    quad_ref[...] = line
    for copy in copies:
        copy.wait()


def border(across, fringe, land, near, far, near_own, far_own, edge, sums, base, half, devices):
    count, variables, _, cols = base.shape
    kernels = fringe.shape[0]
    size = 2 * half * variables
    keep = pl.BlockSpec(memory_space=pl.ANY)
    quads = jax.ShapeDtypeStruct((devices, LANES), F32)
    operands = (across, fringe, land, near, far, near_own, far_own, edge, sums)
    return pl.pallas_call(
        functools.partial(border_kernel, half),
        grid=(1,),
        out_shape=(jax.ShapeDtypeStruct(base.shape, BF16), quads),
        in_specs=[whole(o) for o in operands] + [keep],
        out_specs=(keep, whole(quads)),
        scratch_shapes=[
            pltpu.VMEM((kernels, count, cols // LANES, size, LANES), BF16),
            pltpu.VMEM((count, variables, 2, half, cols), BF16),
            pltpu.SemaphoreType.DMA((2,)),
        ],
        input_output_aliases={len(operands): 0},
        compiler_params=pltpu.CompilerParams(vmem_limit_bytes=32 << 20),
        name="border",
    )(*operands, base)


def per_device(probes, filter_taps, mixing, nugget, land_span):
    count, _, rows, cols = probes.shape
    kernels = filter_taps.shape[0]
    half = filter_taps.shape[2] - 1
    regions, bands = lax.axis_size("region"), lax.axis_size("band")
    inner_pairs = [(i, i ^ 1) for i in range(regions)]
    outer_pairs = [(i, (i + 1 if i % 2 else i - 1) % regions) for i in range(regions)]
    near_pairs = [(i, i ^ 1) for i in range(bands)]
    far_pairs = [(i, i + 1 if i % 2 else i - 1) for i in range(1, bands - 1)]

    probes = pltpu.with_memory_space_constraint(probes, pltpu.HBM)
    span = pltpu.with_memory_space_constraint(land_span.reshape(2, 1, rows), pltpu.HBM)
    outer = pack(probes, span, half, True)
    outer = lax.ppermute(outer, "region", outer_pairs)
    inner = pack(probes, span, half, False)
    inner = lax.ppermute(inner, "region", inner_pairs)
    masked, near, far, land, across, downward, fringe = prepare(probes, filter_taps, mixing, span, half)
    near, far = corner(inner, outer, near, far)
    near_halo = lax.ppermute(near, "band", near_pairs)
    far_halo = lax.ppermute(far, "band", far_pairs)
    base, edge, sums = own(nugget, across, downward, masked, land, inner, outer, half, probes.shape)
    output, quads = border(
        across, fringe, land, near_halo, far_halo, near, far, edge, sums, base, half, regions * bands
    )
    shares = lax.all_to_all(quads, ("region", "band"), 0, 0, tiled=True)
    quadratic = jnp.sum(shares, axis=0)[: count * (kernels + 1)].reshape(count, kernels + 1)
    return output, quadratic / (bands * rows * cols)


def solution(mesh):
    in_specs = (P(None, None, "band", "region"), P(), P(), P(), P(None, "band", "region"))
    out_specs = (P(None, None, "band", "region"), P())
    return jax.shard_map(
        per_device, mesh=mesh, in_specs=in_specs, out_specs=out_specs, check_vma=False
    )
```

time: 41.9 us -> 41.6 us (level)
  waiting for transfers between devices: 1.33 us -> 0.01 us
  Pallas kernels: 17.8 us -> 19 us
    pallas_call x2 -> x3, Pallas kernels: 3.68 us -> 8.3 us  [the longest x2 4.44 us: pack(): pl.pallas_call(functools.partial(pack_kernel, half, cols, outer), grid=(1...]
    pallas_call x1, Pallas kernels: 11.1 us -> 8.11 us  [own(): pl.pallas_call(functools.partial(own_kernel, half), grid=(count,), out_sh...]
    ppermute x1, waiting for transfers between devices: 1.32 us -> 0.01 us  [per_device(): outer = lax.ppermute(outer, 'region', outer_pairs)]
    pallas_call x1, Pallas kernels: 3.1 us -> 2.54 us  [border(): pl.pallas_call(functools.partial(border_kernel, half), grid=(1,), out_sha...]
  transfers between devices with their start and end apart: 4 -> 4, of which waited for: 1 -> 0; matrix products, arithmetic and copies ran while one was open for 0% -> 0% of each run, Pallas kernels for 31% -> 34%
where the time goes in v4:
time: 41.6 us; the launch traced here: 41.3 us
  Pallas kernels  19 us (46%)
  blocking collectives  13.4 us (32%)
  starting transfers between devices  7.44 us (18%)
  between operations  0.74 us (2%)
  local copies, waits for them, and re-layouts  0.68 us (2%)
    all_to_all x1, blocking collectives, per_device(): shares = lax.all_to_all(quads, ('region', 'band'), 0, 0, tiled=True)  13.4 us
    pallas_call x1, Pallas kernels, own(): pl.pallas_call(functools.partial(own_kernel, half), grid=(count,), out_sh...  8.11 us
    pallas_call x2, Pallas kernels, pack(): pl.pallas_call(functools.partial(pack_kernel, half, cols, outer), grid=(1...  4.44 us
    pallas_call x1, Pallas kernels, prepare(): pl.pallas_call(functools.partial(prepare_kernel, half), grid=(count,), ou...  3.86 us
    ppermute x1, starting transfers between devices, per_device(): outer = lax.ppermute(outer, 'region', outer_pairs)  3.64 us
    ppermute x1, starting transfers between devices, per_device(): inner = lax.ppermute(inner, 'region', inner_pairs)  3.03 us
    pallas_call x1, Pallas kernels, border(): pl.pallas_call(functools.partial(border_kernel, half), grid=(1,), out_sha...  2.54 us
  transfers between devices with their start and end apart: 4, of which 0 were waited for; matrix products, arithmetic and copies ran while one was open for 0% of the time, Pallas kernels for 34%

profile of v4, /device:TPU:0, one launch (start us, length us, event | category | flops | bytes accessed | tf_op | source)
XLA Modules:
  0.0 41.3 jit_solution(10472494035271437263)
XLA Ops:
  0.6 0.0 copy-start
  0.6 0.0 copy-start.1
  0.6 2.2 %pack.2 = bf16[2,128,128]{2,1,0:T(8,128)(2,1)S(1)} custom-call(s32[2,1,128]{2,1,0:T(1,128)} %bitcast.5, bf16[4,4,128,1024]{3,2,1,0:T(8,128)(2,1)} %x_ref.5), custom_call_target="tpu_custom_call" | custom-call | flops 1000000 | bytes 1048576 | tf_op jit(solution)/shard_map/pack/pallas_call | solution.py:59
  2.9 0.0 copy-start.2
  2.9 3.0 %collective-permute-start = (bf16[2,128,128]{2,1,0:T(8,128)(2,1)S(1)}, bf16[2,128,128]{2,1,0:T(8,128)(2,1)S(1)}, u32[]{:S(2)}, u32[]{:S(2)}) collective-permute-start(bf16[2,128,128]{2,1,0:T(8,128)(2,1)S(1)} %pack.2), channel_id=1, source_target_pairs={{0,4},{4,0},{8,12},{12,8},{16,20},{20,16},{24,28},{28,24},{1,5},{5... | collective-permute-start | bytes 196616 | tf_op jit(solution)/shard_map/ppermute | solution.py:496
  5.9 2.2 %pack.3 = bf16[2,128,128]{2,1,0:T(8,128)(2,1)S(1)} custom-call(s32[2,1,128]{2,1,0:T(1,128)} %bitcast.6, bf16[4,4,128,1024]{3,2,1,0:T(8,128)(2,1)} %x_ref.5), custom_call_target="tpu_custom_call" | custom-call | flops 1000000 | bytes 1048576 | tf_op jit(solution)/shard_map/pack/pallas_call | solution.py:59
  8.1 3.6 %collective-permute-start.1 = (bf16[2,128,128]{2,1,0:T(8,128)(2,1)S(1)}, bf16[2,128,128]{2,1,0:T(8,128)(2,1)S(1)}, u32[]{:S(2)}, u32[]{:S(2)}) collective-permute-start(bf16[2,128,128]{2,1,0:T(8,128)(2,1)S(1)} %pack.3), channel_id=1, source_target_pairs={{0,28},{4,8},{8,4},{12,16},{16,12},{20,24},{24,20},{28,0},{1,29},{... | collective-permute-start | bytes 196616 | tf_op jit(solution)/shard_map/ppermute | solution.py:494
  11.8 0.0 copy-done
  11.8 0.0 copy-done.1
  11.8 3.9 %prepare.1 = (bf16[16,8,128,128]{3,2,1,0:T(8,128)(2,1)S(1)}, bf16[17,8,16,128]{3,2,1,0:T(8,128)(2,1)S(1)}, bf16[17,8,16,128]{3,2,1,0:T(8,128)(2,1)S(1)}, bf16[8,...) custom-call(f32[2,2,17]{2,1,0:T(2,128)S(1)} %copy-done.1, ...), custom_call_target="tpu_custom_call" | custom-call | flops 10000000 | bytes 4194304 | tf_op jit(solution)/shard_map/prepare/pallas_call | solution.py:177
  15.7 0.0 collective-permute-done.inner_ref
  15.7 0.0 collective-permute-done.1.outer_ref
  15.7 0.1 collective-permute-start.2
  15.8 0.7 %collective-permute-start.3 = (bf16[17,8,16,128]{3,2,1,0:T(8,128)(2,1)S(1)}, bf16[17,8,16,128]{3,2,1,0:T(8,128)(2,1)S(1)}, u32[]{:S(2)}, u32[]{:S(2)}) collective-permute-start(bf16[17,8,16,128]{3,2,1,0:T(8,128)(2,1)S(1)} %get-tuple-element.22.far_own_ref), channel_id=1, source_target_pairs={{1,2},{2,1},{5,6},{6,5},{9,10},{10,9},{13,14},{14,13},{17,18},{18,... | collective-permute-start | bytes 1671176 | tf_op jit(solution)/shard_map/ppermute | solution.py:500
  16.5 0.0 copy-done.2
  16.5 8.1 %own.1 = (bf16[4,4,128,1024]{3,2,1,0:T(8,128)(2,1)}, f32[4,4,2,16,1024]{4,3,2,1,0:T(8,128)S(1)}, f32[4,3,8,128]{3,2,1,0:T(8,128)S(1)}) custom-call(f32[4]{0:T(128)S(1)} %copy-done.2, bf16[256,256]{1,0:T(8,128)(2,1)S(1)} %get-tuple-element.16.across_ref, bf16[2,128,256]{2,1,0:T(8,128)(2,1)S(1)} %get-tuple-element.23.downward_ref, ...), custom_call_target="tpu_custom_call" | custom-call | flops 10000000000 | bytes 16777216 | tf_op jit(solution)/shard_map/own/pallas_call | solution.py:341
  24.6 0.0 collective-permute-done.2.near_ref
  24.6 0.0 collective-permute-done.3.far_ref
  24.6 2.5 %border.1 = (bf16[4,4,128,1024]{3,2,1,0:T(8,128)(2,1)}, f32[32,128]{1,0:T(8,128)S(1)}) custom-call(bf16[256,256]{1,0:T(8,128)(2,1)S(1)} %get-tuple-element.16.across_ref, bf16[2,128,128]{2,1,0:T(8,128)(2,1)S(1)} %get-tuple-element.17.fringe_ref, bf16[8,128,128]{2,1,0:T(8,128)(2,1)S(1)} %get-tuple-element.18.land_ref, ...), custom_call_target="tpu_custom_call", output_to_operand_aliasing={{0}: (9, {})} | custom-call | tf_op jit(solution)/shard_map/border/pallas_call | solution.py:464
  27.2 13.4 %all_to_all.9 = f32[32,1,128]{2,1,0:T(1,128)S(1)} all-to-all(f32[32,1,128]{2,1,0:T(1,128)S(1)} %bitcast.4), channel_id=1, replica_groups=mesh['region'=8,'band'=4] {'region','band'}, dimensions={0} | all-to-all | bytes 32768 | tf_op jit(solution)/shard_map/all_to_all | solution.py:505
  40.5 0.1 reduce_sum.9
  40.6 0.7 %div.6 = f32[4,3]{1,0:T(4,128)} reshape(f32[12]{0:T(128)S(1)} %slice_multiply_fusion) | data formatting | bytes 96 | tf_op jit(solution)/shard_map/div | solution.py:507
  (2 shorter events, 0.0 us)
Async XLA Ops:
  0.6 11.2 %copy-start = (f32[2,4,4]{2,1,0:T(4,128)S(1)}, f32[2,4,4]{2,1,0:T(4,128)}, u32[]{:S(2)}) copy-start(f32[2,4,4]{2,1,0:T(4,128)} %mixing_ref.1) | copy-start | bytes 388
  0.6 11.1 %copy-start.1 = (f32[2,2,17]{2,1,0:T(2,128)S(1)}, f32[2,2,17]{2,1,0:T(2,128)}, u32[]{:S(2)}) copy-start(f32[2,2,17]{2,1,0:T(2,128)} %taps_ref.1) | copy-start | bytes 820
  2.9 13.6 %copy-start.2 = (f32[4]{0:T(128)S(1)}, f32[4]{0:T(128)}, u32[]{:S(2)}) copy-start(f32[4]{0:T(128)} %nugget_ref.1) | copy-start | bytes 52
  2.9 12.8 %collective-permute-start = (bf16[2,128,128]{2,1,0:T(8,128)(2,1)S(1)}, bf16[2,128,128]{2,1,0:T(8,128)(2,1)S(1)}, u32[]{:S(2)}, u32[]{:S(2)}) collective-permute-start(bf16[2,128,128]{2,1,0:T(8,128)(2,1)S(1)} %pack.2), channel_id=1, source_target_pairs={{0,4},{4,0},{8,12},{12,8},{16,20},{20,16},{24,28},{28,24},{1,5},{5... | collective-permute-start | bytes 196616 | tf_op jit(solution)/shard_map/ppermute | solution.py:496
  8.1 7.5 %collective-permute-start.1 = (bf16[2,128,128]{2,1,0:T(8,128)(2,1)S(1)}, bf16[2,128,128]{2,1,0:T(8,128)(2,1)S(1)}, u32[]{:S(2)}, u32[]{:S(2)}) collective-permute-start(bf16[2,128,128]{2,1,0:T(8,128)(2,1)S(1)} %pack.3), channel_id=1, source_target_pairs={{0,28},{4,8},{8,4},{12,16},{16,12},{20,24},{24,20},{28,0},{1,29},{... | collective-permute-start | bytes 196616 | tf_op jit(solution)/shard_map/ppermute | solution.py:494
  15.7 8.9 %collective-permute-start.2 = (bf16[17,8,16,128]{3,2,1,0:T(8,128)(2,1)S(1)}, bf16[17,8,16,128]{3,2,1,0:T(8,128)(2,1)S(1)}, u32[]{:S(2)}, u32[]{:S(2)}) collective-permute-start(bf16[17,8,16,128]{3,2,1,0:T(8,128)(2,1)S(1)} %get-tuple-element.21.near_own_ref), channel_id=1, source_target_pairs={{0,1},{1,0},{2,3},{3,2},{4,5},{5,4},{6,7},{7,6},{8,9},{9,8},{10,11... | collective-permute-start | bytes 1671176 | tf_op jit(solution)/shard_map/ppermute | solution.py:499
  15.8 8.8 %collective-permute-start.3 = (bf16[17,8,16,128]{3,2,1,0:T(8,128)(2,1)S(1)}, bf16[17,8,16,128]{3,2,1,0:T(8,128)(2,1)S(1)}, u32[]{:S(2)}, u32[]{:S(2)}) collective-permute-start(bf16[17,8,16,128]{3,2,1,0:T(8,128)(2,1)S(1)} %get-tuple-element.22.far_own_ref), channel_id=1, source_target_pairs={{1,2},{2,1},{5,6},{6,5},{9,10},{10,9},{13,14},{14,13},{17,18},{18,... | collective-permute-start | bytes 1671176 | tf_op jit(solution)/shard_map/ppermute | solution.py:500

commit v5 on v4

--- a/solution.py
+++ b/solution.py
@@ -35,38 +35,40 @@
     return ((column >= low) & (column < high)).astype(F32).astype(BF16)
 
 
-def pack_kernel(half, cols, outer, span_ref, x_ref, edge_ref, tile_ref, sem):
-    _, variables, _, _ = x_ref.shape
+def pack_kernel(half, cols, span_ref, west_ref, east_ref, inner_ref, outer_ref):
+    variables = west_ref.shape[1]
     per_group = LANES // half
-    east = odd("region") == outer
-    first = pl.multiple_of(jnp.where(east, cols - LANES, 0), LANES)
-    copy = pltpu.make_async_copy(x_ref.at[:, :, :, pl.ds(first, LANES)], tile_ref, sem)
-    copy.start()
     low, high = bounds_by_row(span_ref)
-    land = land_tile(low, high, first)
-    copy.wait()
-    for group in range(edge_ref.shape[0]):
-        pieces = []
+    first = land_tile(low, high, 0)
+    last = land_tile(low, high, cols - LANES)
+    swapped = odd("region")
+    for group in range(inner_ref.shape[0]):
+        heads, tails = [], []
         for plane in range(group * per_group, (group + 1) * per_group):
-            tile = tile_ref[plane // variables, plane % variables] * land
-            pieces.append(jnp.where(east, tile[:, LANES - half :], tile[:, :half]))
-        edge_ref[group] = jnp.concatenate(pieces, axis=1)
-
-
-def pack(probes, span, half, outer):
+            at = (plane // variables, plane % variables)
+            heads.append((west_ref[at] * first)[:, :half])
+            tails.append((east_ref[at] * last)[:, LANES - half :])
+        left, right = jnp.concatenate(heads, axis=1), jnp.concatenate(tails, axis=1)
+        inner_ref[group] = jnp.where(swapped, left, right)
+        outer_ref[group] = jnp.where(swapped, right, left)
+
+
+def pack(probes, span, half):
     count, variables, rows, cols = probes.shape
-    edge = jax.ShapeDtypeStruct((count * variables * half // LANES, rows, LANES), BF16)
+    groups = count * variables * half // LANES
+    steps = 1
+    edge = jax.ShapeDtypeStruct((groups, rows, LANES), BF16)
+    tile = lambda at: pl.BlockSpec((count // steps, variables, rows, LANES), lambda g: (g, 0, 0, at))
+    piece = pl.BlockSpec((groups // steps, rows, LANES), lambda g: (g, 0, 0))
     return pl.pallas_call(
-        functools.partial(pack_kernel, half, cols, outer),
-        grid=(1,),
-        out_shape=edge,
-        in_specs=[whole(span), pl.BlockSpec(memory_space=pl.ANY)],
-        out_specs=whole(edge),
-        scratch_shapes=[pltpu.VMEM((count, variables, rows, LANES), BF16), pltpu.SemaphoreType.DMA],
-        cost_estimate=pl.CostEstimate(flops=10**6, bytes_accessed=1 << 20, transcendentals=0),
+        functools.partial(pack_kernel, half, cols),
+        grid=(steps,),
+        out_shape=(edge, edge),
+        in_specs=[whole(span), tile(0), tile(cols // LANES - 1)],
+        out_specs=(piece, piece),
         compiler_params=pltpu.CompilerParams(vmem_limit_bytes=16 << 20),
         name="pack",
-    )(span, probes)
+    )(span, probes, probes)
 
 
 def prepare_kernel(
@@ -490,9 +492,8 @@
 
     probes = pltpu.with_memory_space_constraint(probes, pltpu.HBM)
     span = pltpu.with_memory_space_constraint(land_span.reshape(2, 1, rows), pltpu.HBM)
-    outer = pack(probes, span, half, True)
+    inner, outer = pack(probes, span, half)
     outer = lax.ppermute(outer, "region", outer_pairs)
-    inner = pack(probes, span, half, False)
     inner = lax.ppermute(inner, "region", inner_pairs)
     masked, near, far, land, across, downward, fringe = prepare(probes, filter_taps, mixing, span, half)
     near, far = corner(inner, outer, near, far)

time: 41.6 us -> 38.7 us (0.930)
  Pallas kernels: 19 us -> 16.4 us
    pallas_call x2 -> x1, Pallas kernels: 4.44 us -> 1.63 us  [pack(): pl.pallas_call(functools.partial(pack_kernel, half, cols), grid=(steps,),...]
  transfers between devices with their start and end apart: 4 -> 4, of which waited for: 0 -> 0; matrix products, arithmetic and copies ran while one was open for 0% -> 0% of each run, Pallas kernels for 34% -> 32%
where the time goes in v5:
time: 38.7 us; the launch traced here: 38.4 us
  Pallas kernels  16.4 us (42%)
  blocking collectives  13.2 us (34%)
  starting transfers between devices  7.37 us (19%)
  between operations  0.73 us (2%)
  local copies, waits for them, and re-layouts  0.68 us (2%)
    all_to_all x1, blocking collectives, per_device(): shares = lax.all_to_all(quads, ('region', 'band'), 0, 0, tiled=True)  13.2 us
    pallas_call x1, Pallas kernels, own(): pl.pallas_call(functools.partial(own_kernel, half), grid=(count,), out_sh...  8.38 us
    pallas_call x1, Pallas kernels, prepare(): pl.pallas_call(functools.partial(prepare_kernel, half), grid=(count,), ou...  3.86 us
    ppermute x1, starting transfers between devices, per_device(): outer = lax.ppermute(outer, 'region', outer_pairs)  3.57 us
    ppermute x1, starting transfers between devices, per_device(): inner = lax.ppermute(inner, 'region', inner_pairs)  3.03 us
    pallas_call x1, Pallas kernels, border(): pl.pallas_call(functools.partial(border_kernel, half), grid=(1,), out_sha...  2.54 us
    pallas_call x1, Pallas kernels, pack(): pl.pallas_call(functools.partial(pack_kernel, half, cols), grid=(steps,),...  1.63 us
  transfers between devices with their start and end apart: 4, of which 0 were waited for; matrix products, arithmetic and copies ran while one was open for 0% of the time, Pallas kernels for 32%

profile of v5, /device:TPU:0, one launch (start us, length us, event | category | flops | bytes accessed | tf_op | source)
XLA Modules:
  0.0 38.4 jit_solution(396164872599738202)
XLA Ops:
  0.6 0.0 copy-start
  0.6 0.0 copy-start.1
  0.6 1.6 %pack.1 = (bf16[2,128,128]{2,1,0:T(8,128)(2,1)S(1)}, bf16[2,128,128]{2,1,0:T(8,128)(2,1)S(1)}) custom-call(s32[2,1,128]{2,1,0:T(1,128)} %bitcast.5, bf16[4,4,128,1024]{3,2,1,0:T(8,128)(2,1)} %east_ref.1, bf16[4,4,128,1024]{3,2,1,0:T(8,128)(2,1)} %east_ref.1), custom_call_target="tpu_custom_call" | custom-call | tf_op jit(solution)/shard_map/pack/pallas_call | solution.py:63
  2.3 0.0 copy-start.2
  2.3 3.0 %collective-permute-start = (bf16[2,128,128]{2,1,0:T(8,128)(2,1)S(1)}, bf16[2,128,128]{2,1,0:T(8,128)(2,1)S(1)}, u32[]{:S(2)}, u32[]{:S(2)}) collective-permute-start(bf16[2,128,128]{2,1,0:T(8,128)(2,1)S(1)} %get-tuple-element.21), channel_id=1, source_target_pairs={{0,4},{4,0},{8,12},{12,8},{16,20},{20,16},{24,28},{28,24},{1,5},{5... | collective-permute-start | bytes 196616 | tf_op jit(solution)/shard_map/ppermute | solution.py:497
  5.3 3.6 %collective-permute-start.1 = (bf16[2,128,128]{2,1,0:T(8,128)(2,1)S(1)}, bf16[2,128,128]{2,1,0:T(8,128)(2,1)S(1)}, u32[]{:S(2)}, u32[]{:S(2)}) collective-permute-start(bf16[2,128,128]{2,1,0:T(8,128)(2,1)S(1)} %get-tuple-element.22), channel_id=1, source_target_pairs={{0,28},{4,8},{8,4},{12,16},{16,12},{20,24},{24,20},{28,0},{1,29},{... | collective-permute-start | bytes 196616 | tf_op jit(solution)/shard_map/ppermute | solution.py:496
  8.9 0.0 copy-done
  8.9 0.0 copy-done.1
  8.9 3.9 %prepare.1 = (bf16[16,8,128,128]{3,2,1,0:T(8,128)(2,1)S(1)}, bf16[17,8,16,128]{3,2,1,0:T(8,128)(2,1)S(1)}, bf16[17,8,16,128]{3,2,1,0:T(8,128)(2,1)S(1)}, bf16[8,...) custom-call(f32[2,2,17]{2,1,0:T(2,128)S(1)} %copy-done.1, ...), custom_call_target="tpu_custom_call" | custom-call | flops 10000000 | bytes 4194304 | tf_op jit(solution)/shard_map/prepare/pallas_call | solution.py:179
  12.8 0.0 collective-permute-done.inner_ref
  12.8 0.0 collective-permute-done.1.outer_ref
  12.8 0.1 collective-permute-start.2
  12.9 0.7 %collective-permute-start.3 = (bf16[17,8,16,128]{3,2,1,0:T(8,128)(2,1)S(1)}, bf16[17,8,16,128]{3,2,1,0:T(8,128)(2,1)S(1)}, u32[]{:S(2)}, u32[]{:S(2)}) collective-permute-start(bf16[17,8,16,128]{3,2,1,0:T(8,128)(2,1)S(1)} %get-tuple-element.26.far_own_ref), channel_id=1, source_target_pairs={{1,2},{2,1},{5,6},{6,5},{9,10},{10,9},{13,14},{14,13},{17,18},{18,... | collective-permute-start | bytes 1671176 | tf_op jit(solution)/shard_map/ppermute | solution.py:501
  13.6 0.0 copy-done.2
  13.6 8.4 %own.1 = (bf16[4,4,128,1024]{3,2,1,0:T(8,128)(2,1)}, f32[4,4,2,16,1024]{4,3,2,1,0:T(8,128)S(1)}, f32[4,3,8,128]{3,2,1,0:T(8,128)S(1)}) custom-call(f32[4]{0:T(128)S(1)} %copy-done.2, bf16[256,256]{1,0:T(8,128)(2,1)S(1)} %get-tuple-element.18.across_ref, bf16[2,128,256]{2,1,0:T(8,128)(2,1)S(1)} %get-tuple-element.27.downward_ref, ...), custom_call_target="tpu_custom_call" | custom-call | flops 10000000000 | bytes 16777216 | tf_op jit(solution)/shard_map/own/pallas_call | solution.py:343
  22.0 0.0 collective-permute-done.2.near_ref
  22.0 0.0 collective-permute-done.3.far_ref
  22.0 2.5 %border.1 = (bf16[4,4,128,1024]{3,2,1,0:T(8,128)(2,1)}, f32[32,128]{1,0:T(8,128)S(1)}) custom-call(bf16[256,256]{1,0:T(8,128)(2,1)S(1)} %get-tuple-element.18.across_ref, bf16[2,128,128]{2,1,0:T(8,128)(2,1)S(1)} %get-tuple-element.19.fringe_ref, bf16[8,128,128]{2,1,0:T(8,128)(2,1)S(1)} %get-tuple-element.20.land_ref, ...), custom_call_target="tpu_custom_call", output_to_operand_aliasing={{0}: (9, {})} | custom-call | tf_op jit(solution)/shard_map/border/pallas_call | solution.py:466
  24.6 13.2 %all_to_all.9 = f32[32,1,128]{2,1,0:T(1,128)S(1)} all-to-all(f32[32,1,128]{2,1,0:T(1,128)S(1)} %bitcast.4), channel_id=1, replica_groups=mesh['region'=8,'band'=4] {'region','band'}, dimensions={0} | all-to-all | bytes 32768 | tf_op jit(solution)/shard_map/all_to_all | solution.py:506
  37.7 0.1 reduce_sum.9
  37.8 0.7 %div.6 = f32[4,3]{1,0:T(4,128)} reshape(f32[12]{0:T(128)S(1)} %slice_multiply_fusion) | data formatting | bytes 96 | tf_op jit(solution)/shard_map/div | solution.py:508
  (2 shorter events, 0.0 us)
Async XLA Ops:
  0.6 8.3 %copy-start = (f32[2,4,4]{2,1,0:T(4,128)S(1)}, f32[2,4,4]{2,1,0:T(4,128)}, u32[]{:S(2)}) copy-start(f32[2,4,4]{2,1,0:T(4,128)} %mixing_ref.1) | copy-start | bytes 388
  0.6 8.3 %copy-start.1 = (f32[2,2,17]{2,1,0:T(2,128)S(1)}, f32[2,2,17]{2,1,0:T(2,128)}, u32[]{:S(2)}) copy-start(f32[2,2,17]{2,1,0:T(2,128)} %taps_ref.1) | copy-start | bytes 820
  2.3 11.3 %copy-start.2 = (f32[4]{0:T(128)S(1)}, f32[4]{0:T(128)}, u32[]{:S(2)}) copy-start(f32[4]{0:T(128)} %nugget_ref.1) | copy-start | bytes 52
  2.3 10.5 %collective-permute-start = (bf16[2,128,128]{2,1,0:T(8,128)(2,1)S(1)}, bf16[2,128,128]{2,1,0:T(8,128)(2,1)S(1)}, u32[]{:S(2)}, u32[]{:S(2)}) collective-permute-start(bf16[2,128,128]{2,1,0:T(8,128)(2,1)S(1)} %get-tuple-element.21), channel_id=1, source_target_pairs={{0,4},{4,0},{8,12},{12,8},{16,20},{20,16},{24,28},{28,24},{1,5},{5... | collective-permute-start | bytes 196616 | tf_op jit(solution)/shard_map/ppermute | solution.py:497
  5.3 7.5 %collective-permute-start.1 = (bf16[2,128,128]{2,1,0:T(8,128)(2,1)S(1)}, bf16[2,128,128]{2,1,0:T(8,128)(2,1)S(1)}, u32[]{:S(2)}, u32[]{:S(2)}) collective-permute-start(bf16[2,128,128]{2,1,0:T(8,128)(2,1)S(1)} %get-tuple-element.22), channel_id=1, source_target_pairs={{0,28},{4,8},{8,4},{12,16},{16,12},{20,24},{24,20},{28,0},{1,29},{... | collective-permute-start | bytes 196616 | tf_op jit(solution)/shard_map/ppermute | solution.py:496
  12.8 9.2 %collective-permute-start.2 = (bf16[17,8,16,128]{3,2,1,0:T(8,128)(2,1)S(1)}, bf16[17,8,16,128]{3,2,1,0:T(8,128)(2,1)S(1)}, u32[]{:S(2)}, u32[]{:S(2)}) collective-permute-start(bf16[17,8,16,128]{3,2,1,0:T(8,128)(2,1)S(1)} %get-tuple-element.25.near_own_ref), channel_id=1, source_target_pairs={{0,1},{1,0},{2,3},{3,2},{4,5},{5,4},{6,7},{7,6},{8,9},{9,8},{10,11... | collective-permute-start | bytes 1671176 | tf_op jit(solution)/shard_map/ppermute | solution.py:500
  12.9 9.1 %collective-permute-start.3 = (bf16[17,8,16,128]{3,2,1,0:T(8,128)(2,1)S(1)}, bf16[17,8,16,128]{3,2,1,0:T(8,128)(2,1)S(1)}, u32[]{:S(2)}, u32[]{:S(2)}) collective-permute-start(bf16[17,8,16,128]{3,2,1,0:T(8,128)(2,1)S(1)} %get-tuple-element.26.far_own_ref), channel_id=1, source_target_pairs={{1,2},{2,1},{5,6},{6,5},{9,10},{10,9},{13,14},{14,13},{17,18},{18,... | collective-permute-start | bytes 1671176 | tf_op jit(solution)/shard_map/ppermute | solution.py:501

commit v6 on v5

--- a/solution.py
+++ b/solution.py
@@ -38,17 +38,32 @@
 def pack_kernel(half, cols, span_ref, west_ref, east_ref, inner_ref, outer_ref):
     variables = west_ref.shape[1]
     per_group = LANES // half
+    swapped = odd("region")
     low, high = bounds_by_row(span_ref)
-    first = land_tile(low, high, 0)
-    last = land_tile(low, high, cols - LANES)
-    swapped = odd("region")
+    lane = lax.broadcasted_iota(jnp.int32, low.shape, 1)
+    column = (lane & (half - 1)).astype(F32)
+    first = ((column >= low) & (column < high)).astype(F32).astype(BF16)
+    column = column + (cols - half)
+    last = ((column >= low) & (column < high)).astype(F32).astype(BF16)
     for group in range(inner_ref.shape[0]):
-        heads, tails = [], []
-        for plane in range(group * per_group, (group + 1) * per_group):
-            at = (plane // variables, plane % variables)
-            heads.append((west_ref[at] * first)[:, :half])
-            tails.append((east_ref[at] * last)[:, LANES - half :])
-        left, right = jnp.concatenate(heads, axis=1), jnp.concatenate(tails, axis=1)
+        left = right = None
+        for k in range(per_group + 1):
+            plane = group * per_group + k
+            west = west_ref[plane // variables, plane % variables] if k < per_group else None
+            plane -= 1
+            east = east_ref[plane // variables, plane % variables] if k > 0 else None
+            if east is None:
+                both = west
+            elif west is None:
+                both = east
+            else:
+                both = jnp.where(lane < LANES // 2, west, east)
+                both = pltpu.roll(both, k * half, 1)
+            if west is not None:
+                left = both if left is None else jnp.where(lane < k * half, left, both)
+            if east is not None:
+                right = both if right is None else jnp.where(lane < (k - 1) * half, right, both)
+        left, right = left * first, right * last
         inner_ref[group] = jnp.where(swapped, left, right)
         outer_ref[group] = jnp.where(swapped, right, left)
 
@@ -317,9 +332,9 @@
                     total = total + term
                 out_ref[0, v, here, span] = total.astype(BF16) * land
                 if first == 0:
-                    edge_ref[0, v, upper, :, span] = total[:half]
+                    edge_ref[probe, v, upper, :, span] = total[:half]
                 if first + step == rows:
-                    edge_ref[0, v, 1 - upper, :, span] = total[step - half :]
+                    edge_ref[probe, v, 1 - upper, :, span] = total[step - half :]
 
     filter_columns(0)
     for chunk in range(cols // wide):
@@ -327,7 +342,7 @@
             filter_columns(chunk + 1)
         filter_rows(chunk)
     for k in range(kernels + 1):
-        sums_ref[0, k] = sums[k]
+        sums_ref[probe, k] = sums[k]
 
 
 def own(nugget, across, downward, masked, land, inner, outer, half, shape):
@@ -345,7 +360,7 @@
         grid=(count,),
         out_shape=outs,
         in_specs=[SMEM] + [whole(o) for o in operands],
-        out_specs=tuple(block(*o.shape[1:]) for o in outs),
+        out_specs=(block(*shape[1:]), whole(outs[1]), whole(outs[2])),
         scratch_shapes=[pltpu.VMEM((kernels, variables, cols // LANES, rows + 2 * half, LANES), BF16)],
         cost_estimate=pl.CostEstimate(flops=10**10, bytes_accessed=16 << 20, transcendentals=0),
         compiler_params=pltpu.CompilerParams(vmem_limit_bytes=32 << 20),

time: 38.7 us -> 38.5 us (level)
  no operation moved by 1% of the time
where the time goes in v6:
time: 38.5 us; the launch traced here: 38.3 us
  Pallas kernels  16.3 us (42%)
  blocking collectives  13.2 us (34%)
  starting transfers between devices  7.37 us (19%)
  between operations  0.73 us (2%)
  local copies, waits for them, and re-layouts  0.68 us (2%)
    all_to_all x1, blocking collectives, per_device(): shares = lax.all_to_all(quads, ('region', 'band'), 0, 0, tiled=True)  13.2 us
    pallas_call x1, Pallas kernels, own(): pl.pallas_call(functools.partial(own_kernel, half), grid=(count,), out_sh...  8.38 us
    pallas_call x1, Pallas kernels, prepare(): pl.pallas_call(functools.partial(prepare_kernel, half), grid=(count,), ou...  3.86 us
    ppermute x1, starting transfers between devices, per_device(): outer = lax.ppermute(outer, 'region', outer_pairs)  3.57 us
    ppermute x1, starting transfers between devices, per_device(): inner = lax.ppermute(inner, 'region', inner_pairs)  3.03 us
    pallas_call x1, Pallas kernels, border(): pl.pallas_call(functools.partial(border_kernel, half), grid=(1,), out_sha...  2.54 us
    pallas_call x1, Pallas kernels, pack(): pl.pallas_call(functools.partial(pack_kernel, half, cols), grid=(steps,),...  1.5 us
  transfers between devices with their start and end apart: 4, of which 0 were waited for; matrix products, arithmetic and copies ran while one was open for 0% of the time, Pallas kernels for 32%

profile of v6, /device:TPU:0, one launch (start us, length us, event | category | flops | bytes accessed | tf_op | source)
XLA Modules:
  0.0 38.3 jit_solution(18274171165955471260)
XLA Ops:
  0.6 0.0 copy-start
  0.6 0.0 copy-start.1
  0.6 1.5 %pack.1 = (bf16[2,128,128]{2,1,0:T(8,128)(2,1)S(1)}, bf16[2,128,128]{2,1,0:T(8,128)(2,1)S(1)}) custom-call(s32[2,1,128]{2,1,0:T(1,128)} %bitcast.5, bf16[4,4,128,1024]{3,2,1,0:T(8,128)(2,1)} %east_ref.1, bf16[4,4,128,1024]{3,2,1,0:T(8,128)(2,1)} %east_ref.1), custom_call_target="tpu_custom_call" | custom-call | tf_op jit(solution)/shard_map/pack/pallas_call | solution.py:78
  2.2 0.0 copy-start.2
  2.2 3.0 %collective-permute-start = (bf16[2,128,128]{2,1,0:T(8,128)(2,1)S(1)}, bf16[2,128,128]{2,1,0:T(8,128)(2,1)S(1)}, u32[]{:S(2)}, u32[]{:S(2)}) collective-permute-start(bf16[2,128,128]{2,1,0:T(8,128)(2,1)S(1)} %get-tuple-element.21), channel_id=1, source_target_pairs={{0,4},{4,0},{8,12},{12,8},{16,20},{20,16},{24,28},{28,24},{1,5},{5... | collective-permute-start | bytes 196616 | tf_op jit(solution)/shard_map/ppermute | solution.py:512
  5.2 3.6 %collective-permute-start.1 = (bf16[2,128,128]{2,1,0:T(8,128)(2,1)S(1)}, bf16[2,128,128]{2,1,0:T(8,128)(2,1)S(1)}, u32[]{:S(2)}, u32[]{:S(2)}) collective-permute-start(bf16[2,128,128]{2,1,0:T(8,128)(2,1)S(1)} %get-tuple-element.22), channel_id=1, source_target_pairs={{0,28},{4,8},{8,4},{12,16},{16,12},{20,24},{24,20},{28,0},{1,29},{... | collective-permute-start | bytes 196616 | tf_op jit(solution)/shard_map/ppermute | solution.py:511
  8.8 0.0 copy-done
  8.8 0.0 copy-done.1
  8.8 3.9 %prepare.1 = (bf16[16,8,128,128]{3,2,1,0:T(8,128)(2,1)S(1)}, bf16[17,8,16,128]{3,2,1,0:T(8,128)(2,1)S(1)}, bf16[17,8,16,128]{3,2,1,0:T(8,128)(2,1)S(1)}, bf16[8,...) custom-call(f32[2,2,17]{2,1,0:T(2,128)S(1)} %copy-done.1, ...), custom_call_target="tpu_custom_call" | custom-call | flops 10000000 | bytes 4194304 | tf_op jit(solution)/shard_map/prepare/pallas_call | solution.py:194
  12.7 0.0 collective-permute-done.inner_ref
  12.7 0.0 collective-permute-done.1.outer_ref
  12.7 0.1 collective-permute-start.2
  12.8 0.7 %collective-permute-start.3 = (bf16[17,8,16,128]{3,2,1,0:T(8,128)(2,1)S(1)}, bf16[17,8,16,128]{3,2,1,0:T(8,128)(2,1)S(1)}, u32[]{:S(2)}, u32[]{:S(2)}) collective-permute-start(bf16[17,8,16,128]{3,2,1,0:T(8,128)(2,1)S(1)} %get-tuple-element.26.far_own_ref), channel_id=1, source_target_pairs={{1,2},{2,1},{5,6},{6,5},{9,10},{10,9},{13,14},{14,13},{17,18},{18,... | collective-permute-start | bytes 1671176 | tf_op jit(solution)/shard_map/ppermute | solution.py:516
  13.5 0.0 copy-done.2
  13.5 8.4 %own.1 = (bf16[4,4,128,1024]{3,2,1,0:T(8,128)(2,1)}, f32[4,4,2,16,1024]{4,3,2,1,0:T(8,128)S(1)}, f32[4,3,8,128]{3,2,1,0:T(8,128)S(1)}) custom-call(f32[4]{0:T(128)S(1)} %copy-done.2, bf16[256,256]{1,0:T(8,128)(2,1)S(1)} %get-tuple-element.18.across_ref, bf16[2,128,256]{2,1,0:T(8,128)(2,1)S(1)} %get-tuple-element.27.downward_ref, ...), custom_call_target="tpu_custom_call" | custom-call | flops 10000000000 | bytes 16777216 | tf_op jit(solution)/shard_map/own/pallas_call | solution.py:358
  21.9 0.0 collective-permute-done.2.near_ref
  21.9 0.0 collective-permute-done.3.far_ref
  21.9 2.5 %border.1 = (bf16[4,4,128,1024]{3,2,1,0:T(8,128)(2,1)}, f32[32,128]{1,0:T(8,128)S(1)}) custom-call(bf16[256,256]{1,0:T(8,128)(2,1)S(1)} %get-tuple-element.18.across_ref, bf16[2,128,128]{2,1,0:T(8,128)(2,1)S(1)} %get-tuple-element.19.fringe_ref, bf16[8,128,128]{2,1,0:T(8,128)(2,1)S(1)} %get-tuple-element.20.land_ref, ...), custom_call_target="tpu_custom_call", output_to_operand_aliasing={{0}: (9, {})} | custom-call | tf_op jit(solution)/shard_map/border/pallas_call | solution.py:481
  24.4 13.2 %all_to_all.9 = f32[32,1,128]{2,1,0:T(1,128)S(1)} all-to-all(f32[32,1,128]{2,1,0:T(1,128)S(1)} %bitcast.4), channel_id=1, replica_groups=mesh['region'=8,'band'=4] {'region','band'}, dimensions={0} | all-to-all | bytes 32768 | tf_op jit(solution)/shard_map/all_to_all | solution.py:521
  37.6 0.1 reduce_sum.9
  37.7 0.7 %div.6 = f32[4,3]{1,0:T(4,128)} reshape(f32[12]{0:T(128)S(1)} %slice_multiply_fusion) | data formatting | bytes 96 | tf_op jit(solution)/shard_map/div | solution.py:523
  (2 shorter events, 0.0 us)
Async XLA Ops:
  0.6 8.1 %copy-start = (f32[2,4,4]{2,1,0:T(4,128)S(1)}, f32[2,4,4]{2,1,0:T(4,128)}, u32[]{:S(2)}) copy-start(f32[2,4,4]{2,1,0:T(4,128)} %mixing_ref.1) | copy-start | bytes 388
  0.6 8.1 %copy-start.1 = (f32[2,2,17]{2,1,0:T(2,128)S(1)}, f32[2,2,17]{2,1,0:T(2,128)}, u32[]{:S(2)}) copy-start(f32[2,2,17]{2,1,0:T(2,128)} %taps_ref.1) | copy-start | bytes 820
  2.2 11.3 %copy-start.2 = (f32[4]{0:T(128)S(1)}, f32[4]{0:T(128)}, u32[]{:S(2)}) copy-start(f32[4]{0:T(128)} %nugget_ref.1) | copy-start | bytes 52
  2.2 10.5 %collective-permute-start = (bf16[2,128,128]{2,1,0:T(8,128)(2,1)S(1)}, bf16[2,128,128]{2,1,0:T(8,128)(2,1)S(1)}, u32[]{:S(2)}, u32[]{:S(2)}) collective-permute-start(bf16[2,128,128]{2,1,0:T(8,128)(2,1)S(1)} %get-tuple-element.21), channel_id=1, source_target_pairs={{0,4},{4,0},{8,12},{12,8},{16,20},{20,16},{24,28},{28,24},{1,5},{5... | collective-permute-start | bytes 196616 | tf_op jit(solution)/shard_map/ppermute | solution.py:512
  5.2 7.5 %collective-permute-start.1 = (bf16[2,128,128]{2,1,0:T(8,128)(2,1)S(1)}, bf16[2,128,128]{2,1,0:T(8,128)(2,1)S(1)}, u32[]{:S(2)}, u32[]{:S(2)}) collective-permute-start(bf16[2,128,128]{2,1,0:T(8,128)(2,1)S(1)} %get-tuple-element.22), channel_id=1, source_target_pairs={{0,28},{4,8},{8,4},{12,16},{16,12},{20,24},{24,20},{28,0},{1,29},{... | collective-permute-start | bytes 196616 | tf_op jit(solution)/shard_map/ppermute | solution.py:511
  12.7 9.2 %collective-permute-start.2 = (bf16[17,8,16,128]{3,2,1,0:T(8,128)(2,1)S(1)}, bf16[17,8,16,128]{3,2,1,0:T(8,128)(2,1)S(1)}, u32[]{:S(2)}, u32[]{:S(2)}) collective-permute-start(bf16[17,8,16,128]{3,2,1,0:T(8,128)(2,1)S(1)} %get-tuple-element.25.near_own_ref), channel_id=1, source_target_pairs={{0,1},{1,0},{2,3},{3,2},{4,5},{5,4},{6,7},{7,6},{8,9},{9,8},{10,11... | collective-permute-start | bytes 1671176 | tf_op jit(solution)/shard_map/ppermute | solution.py:515
  12.8 9.1 %collective-permute-start.3 = (bf16[17,8,16,128]{3,2,1,0:T(8,128)(2,1)S(1)}, bf16[17,8,16,128]{3,2,1,0:T(8,128)(2,1)S(1)}, u32[]{:S(2)}, u32[]{:S(2)}) collective-permute-start(bf16[17,8,16,128]{3,2,1,0:T(8,128)(2,1)S(1)} %get-tuple-element.26.far_own_ref), channel_id=1, source_target_pairs={{1,2},{2,1},{5,6},{6,5},{9,10},{10,9},{13,14},{14,13},{17,18},{18,... | collective-permute-start | bytes 1671176 | tf_op jit(solution)/shard_map/ppermute | solution.py:516
